TPU v7x, 32 devices: a whole 2x2x4 slice. The times are simulated.
32 devices in a mesh: shard: 8 (over z, x), seq: 4 (over y, core).
Axes of the slice: x: 2, y: 2, z: 4, core: 2. Of those that a mesh axis runs over, the one named last changes fastest.
Arguments:
- inputs: bfloat16 [16, 512, 768], P('shard', 'seq'), may hold values from -6 to 6
- lengths: int32 [16], P('shard'), may hold values from 128 to 512, as said below
- w_query: bfloat16 [768, 768], P('shard'), may hold values from -0.21875 to 0.21875
- b_query: bfloat16 [768], P('shard'), may hold values from -3 to 3
- w_key: bfloat16 [768, 768], P('shard'), may hold values from -0.21875 to 0.21875
- w_value: bfloat16 [768, 768], P('shard'), may hold values from -0.21875 to 0.21875
- b_value: bfloat16 [768], P('shard'), may hold values from -2 to 2
- w_output: bfloat16 [768, 768], P('shard'), may hold values from -0.875 to 0.875
- b_output: bfloat16 [768], P('shard'), may hold values from -2 to 2
- gain_one: bfloat16 [768], P('shard'), may hold values from 0.25 to 1.75
- shift_one: bfloat16 [768], P('shard'), may hold values from -2 to 2
- w_inner: bfloat16 [768, 3072], P('shard'), may hold values from -0.21875 to 0.21875
- b_inner: bfloat16 [3072], P('shard'), may hold values from -2 to 2
- w_outer: bfloat16 [3072, 768], P('shard'), may hold values from -0.109375 to 0.109375
- b_outer: bfloat16 [768], P('shard'), may hold values from -2 to 2
- gain_two: bfloat16 [768], P('shard'), may hold values from 0.25 to 1.75
- shift_two: bfloat16 [768], P('shard'), may hold values from -2 to 2
- cotangent: bfloat16 [16, 512, 768], P('shard', 'seq'), may hold values from -6 to 6
Outputs:
- output: bfloat16 [16, 512, 768], P('shard', 'seq')
- grad_inputs: float32 [16, 512, 768], P('shard', 'seq')
- grad_w_query: float32 [768, 768], P('shard')
- grad_b_query: float32 [768], P('shard')
- grad_w_key: float32 [768, 768], P('shard')
- grad_w_value: float32 [768, 768], P('shard')
- grad_b_value: float32 [768], P('shard')
- grad_w_output: float32 [768, 768], P('shard')
- grad_b_output: float32 [768], P('shard')
- grad_gain_one: float32 [768], P('shard')
- grad_shift_one: float32 [768], P('shard')
- grad_w_inner: float32 [768, 3072], P('shard')
- grad_b_inner: float32 [3072], P('shard')
- grad_w_outer: float32 [3072, 768], P('shard')
- grad_b_outer: float32 [768], P('shard')
- grad_gain_two: float32 [768], P('shard')
- grad_shift_two: float32 [768], P('shard')
Inputs may be any that keep to these rules, and one draw needn't show every extreme that they name: `lengths`: every draw has a slot of 512 valid tokens and a slot of 128.
All inputs are finite; a program needn't handle non-finite values.
Results may differ from a plain program's by a relative error of at most 0.017.
Values may be sent and summed in bfloat16 or wider, within the bound.
A program may use at most 128 MiB of HBM per device.

v0:
```python
from functools import partial

import jax
import jax.numpy as jnp
from jax import lax
from jax.sharding import PartitionSpec as P

HEAD_DIM = 64


epsilon = 1e-12


def layer_norm(tensor, norm_gain, norm_shift):
    average = jnp.mean(tensor, axis=-1, keepdims=True)
    centred = tensor - average
    variance = jnp.mean(centred * centred, axis=-1, keepdims=True)
    return centred * lax.rsqrt(variance + epsilon) * norm_gain + norm_shift


def product(operand, weight):
    return jnp.dot(operand, weight, preferred_element_type=jnp.float32)


def row_contract(operand, weight):
    return lax.dot_general(
        operand, weight, (((0,), (0,)), ((), ())), preferred_element_type=jnp.float32
    )


def times_transposed(operand, weight):
    return lax.dot_general(
        operand, weight, (((1,), (1,)), ((), ())), preferred_element_type=jnp.float32
    )


def column_sum(tensor):
    return jnp.sum(tensor.astype(jnp.float32), axis=0)


def head_logits(query_seq, key_seq, length, factor):
    scores = (
        jnp.einsum("qhd,khd->hqk", query_seq, key_seq, preferred_element_type=jnp.float32) * factor
    )
    visible = jnp.arange(key_seq.shape[0]) < length
    return jnp.where(visible[None, None, :], scores, -1000000000.0)


def per_device(
    inputs,
    lengths,
    w_query,
    b_query,
    w_key,
    w_value,
    b_value,
    w_output,
    b_output,
    gain_one,
    shift_one,
    w_inner,
    b_inner,
    w_outer,
    b_outer,
    gain_two,
    shift_two,
    cotangent,
):
    local_seqs, tok_dev, model_width = inputs.shape
    groups = lax.axis_size("seq")
    head_width = model_width // groups
    local_heads = head_width // HEAD_DIM
    factor = HEAD_DIM ** (-0.5)
    gathered = (
        lax.all_gather(w_query, "shard", axis=0, tiled=True),
        lax.all_gather(b_query, "shard", axis=0, tiled=True),
        lax.all_gather(w_key, "shard", axis=0, tiled=True),
        lax.all_gather(w_value, "shard", axis=0, tiled=True),
        lax.all_gather(b_value, "shard", axis=0, tiled=True),
        lax.all_gather(w_output, "shard", axis=0, tiled=True),
        lax.all_gather(b_output, "shard", axis=0, tiled=True),
        lax.all_gather(gain_one, "shard", axis=0, tiled=True),
        lax.all_gather(shift_one, "shard", axis=0, tiled=True),
        lax.all_gather(w_inner, "shard", axis=0, tiled=True),
        lax.all_gather(b_inner, "shard", axis=0, tiled=True),
        lax.all_gather(w_outer, "shard", axis=0, tiled=True),
        lax.all_gather(b_outer, "shard", axis=0, tiled=True),
        lax.all_gather(gain_two, "shard", axis=0, tiled=True),
        lax.all_gather(shift_two, "shard", axis=0, tiled=True),
    )
    (
        query_w,
        query_b,
        key_w,
        value_w,
        value_b,
        output_w,
        output_b,
        gain_a,
        shift_a,
        inner_w,
        inner_b,
        outer_w,
        outer_b,
        gain_b,
        shift_b,
    ) = gathered
    gain_first = gain_a.astype(jnp.float32)
    shift_first = shift_a.astype(jnp.float32)
    gain_second = gain_b.astype(jnp.float32)
    shift_second = shift_b.astype(jnp.float32)
    flat_rows = inputs.reshape(local_seqs * tok_dev, model_width)
    queries = (product(flat_rows, query_w) + query_b.astype(jnp.float32)).astype(jnp.bfloat16)
    key_rows = product(flat_rows, key_w).astype(jnp.bfloat16)
    values = (product(flat_rows, value_w) + value_b.astype(jnp.float32)).astype(jnp.bfloat16)
    shape_seq = (local_seqs, tok_dev, model_width)
    head_q, head_k, head_v = (
        lax.all_to_all(queries.reshape(shape_seq), "seq", split_axis=2, concat_axis=1, tiled=True),
        lax.all_to_all(key_rows.reshape(shape_seq), "seq", split_axis=2, concat_axis=1, tiled=True),
        lax.all_to_all(values.reshape(shape_seq), "seq", split_axis=2, concat_axis=1, tiled=True),
    )
    seq_len = head_q.shape[1]
    split = (local_seqs, seq_len, local_heads, HEAD_DIM)
    head_q = head_q.reshape(split)
    head_k = head_k.reshape(split)
    head_v = head_v.reshape(split)

    def attend(packed):
        query_seq, key_seq, value_seq, length = packed
        logits = head_logits(query_seq, key_seq, length, factor)
        row_max = jnp.max(logits, axis=-1, keepdims=True)
        shifted = jnp.exp(logits - row_max)
        row_total = jnp.sum(shifted, axis=-1, keepdims=True)
        weights = (shifted / row_total).astype(jnp.bfloat16)
        context = jnp.einsum("hqk,khd->qhd", weights, value_seq, preferred_element_type=jnp.float32)
        return (context.astype(jnp.bfloat16), (row_max + jnp.log(row_total))[..., 0])

    head_context, log_total = lax.map(attend, (head_q, head_k, head_v, lengths))
    back_shape = (local_seqs, seq_len, head_width)
    context = lax.all_to_all(
        head_context.reshape(back_shape), "seq", split_axis=1, concat_axis=2, tiled=True
    ).reshape(-1, model_width)
    branch = product(context, output_w) + output_b.astype(jnp.float32)
    summed = flat_rows.astype(jnp.float32) + branch
    normed = layer_norm(summed, gain_first, shift_first)
    normed_low = normed.astype(jnp.bfloat16)
    pre_inner = product(normed_low, inner_w) + inner_b.astype(jnp.float32)
    activated = jax.nn.gelu(pre_inner, approximate=False).astype(jnp.bfloat16)
    final_sum = normed + product(activated, outer_w) + outer_b.astype(jnp.float32)
    result = layer_norm(final_sum, gain_second, shift_second)
    grad_out = cotangent.reshape(-1, model_width).astype(jnp.float32)
    second_back = jax.vjp(layer_norm, final_sum, gain_second, shift_second)[1]
    grad_final, grad_gain_two, grad_shift_two = second_back(grad_out)
    grad_ffn = grad_final.astype(jnp.bfloat16)
    grad_w_outer = row_contract(activated, grad_ffn)
    grad_b_outer = column_sum(grad_ffn)
    grad_active = times_transposed(grad_ffn, outer_w)
    gelu_back = jax.vjp(partial(jax.nn.gelu, approximate=False), pre_inner)[1]
    grad_pre = gelu_back(grad_active)[0].astype(jnp.bfloat16)
    grad_w_inner = row_contract(normed_low, grad_pre)
    grad_b_inner = column_sum(grad_pre)
    grad_normed = grad_final + times_transposed(grad_pre, inner_w)
    first_back = jax.vjp(layer_norm, summed, gain_first, shift_first)[1]
    grad_summed, grad_gain_one, grad_shift_one = first_back(grad_normed)
    grad_branch = grad_summed.astype(jnp.bfloat16)
    grad_w_output = row_contract(context, grad_branch)
    grad_b_output = column_sum(grad_branch)
    grad_context = times_transposed(grad_branch, output_w).astype(jnp.bfloat16)
    grad_head_context = lax.all_to_all(
        grad_context.reshape(shape_seq), "seq", split_axis=2, concat_axis=1, tiled=True
    ).reshape(split)

    def attend_back(packed):
        query_seq, key_seq, value_seq, log_sum, grad_seq, length = packed
        logits = head_logits(query_seq, key_seq, length, factor)
        attn_probs = jnp.exp(logits - log_sum[..., None])
        weights = attn_probs.astype(jnp.bfloat16)
        grad_value = jnp.einsum(
            "hqk,qhd->khd", weights, grad_seq, preferred_element_type=jnp.float32
        )
        grad_probs = jnp.einsum(
            "qhd,khd->hqk", grad_seq, value_seq, preferred_element_type=jnp.float32
        )
        inner_sum = jnp.sum(grad_probs * attn_probs, axis=-1, keepdims=True)
        grad_scores = (attn_probs * (grad_probs - inner_sum)).astype(jnp.bfloat16)
        grad_query = (
            jnp.einsum("hqk,khd->qhd", grad_scores, key_seq, preferred_element_type=jnp.float32)
            * factor
        )
        grad_key = (
            jnp.einsum("hqk,qhd->khd", grad_scores, query_seq, preferred_element_type=jnp.float32)
            * factor
        )
        return (
            grad_query.astype(jnp.bfloat16),
            grad_key.astype(jnp.bfloat16),
            grad_value.astype(jnp.bfloat16),
        )

    head_gq, head_gk, head_gv = lax.map(
        attend_back, (head_q, head_k, head_v, log_total, grad_head_context, lengths)
    )
    tok_gq, tok_gk, tok_gv = (
        lax.all_to_all(head_gq.reshape(back_shape), "seq", split_axis=1, concat_axis=2, tiled=True),
        lax.all_to_all(head_gk.reshape(back_shape), "seq", split_axis=1, concat_axis=2, tiled=True),
        lax.all_to_all(head_gv.reshape(back_shape), "seq", split_axis=1, concat_axis=2, tiled=True),
    )
    grad_query = tok_gq.reshape(-1, model_width)
    grad_key = tok_gk.reshape(-1, model_width)
    grad_value = tok_gv.reshape(-1, model_width)
    grad_w_query = row_contract(flat_rows, grad_query)
    grad_b_query = column_sum(grad_query)
    grad_w_key = row_contract(flat_rows, grad_key)
    grad_w_value = row_contract(flat_rows, grad_value)
    grad_b_value = column_sum(grad_value)
    grad_rows = (
        grad_summed
        + times_transposed(grad_query, query_w)
        + times_transposed(grad_key, key_w)
        + times_transposed(grad_value, value_w)
    )
    local_grads = (
        grad_w_query,
        grad_b_query,
        grad_w_key,
        grad_w_value,
        grad_b_value,
        grad_w_output,
        grad_b_output,
        grad_gain_one,
        grad_shift_one,
        grad_w_inner,
        grad_b_inner,
        grad_w_outer,
        grad_b_outer,
        grad_gain_two,
        grad_shift_two,
    )
    shares = (
        lax.psum_scatter(local_grads[0], "shard", scatter_dimension=0, tiled=True),
        lax.psum_scatter(local_grads[1], "shard", scatter_dimension=0, tiled=True),
        lax.psum_scatter(local_grads[2], "shard", scatter_dimension=0, tiled=True),
        lax.psum_scatter(local_grads[3], "shard", scatter_dimension=0, tiled=True),
        lax.psum_scatter(local_grads[4], "shard", scatter_dimension=0, tiled=True),
        lax.psum_scatter(local_grads[5], "shard", scatter_dimension=0, tiled=True),
        lax.psum_scatter(local_grads[6], "shard", scatter_dimension=0, tiled=True),
        lax.psum_scatter(local_grads[7], "shard", scatter_dimension=0, tiled=True),
        lax.psum_scatter(local_grads[8], "shard", scatter_dimension=0, tiled=True),
        lax.psum_scatter(local_grads[9], "shard", scatter_dimension=0, tiled=True),
        lax.psum_scatter(local_grads[10], "shard", scatter_dimension=0, tiled=True),
        lax.psum_scatter(local_grads[11], "shard", scatter_dimension=0, tiled=True),
        lax.psum_scatter(local_grads[12], "shard", scatter_dimension=0, tiled=True),
        lax.psum_scatter(local_grads[13], "shard", scatter_dimension=0, tiled=True),
        lax.psum_scatter(local_grads[14], "shard", scatter_dimension=0, tiled=True),
    )
    summed_grads = (
        lax.psum(shares[0].astype(jnp.bfloat16), "seq").astype(jnp.float32),
        lax.psum(shares[1].astype(jnp.bfloat16), "seq").astype(jnp.float32),
        lax.psum(shares[2].astype(jnp.bfloat16), "seq").astype(jnp.float32),
        lax.psum(shares[3].astype(jnp.bfloat16), "seq").astype(jnp.float32),
        lax.psum(shares[4].astype(jnp.bfloat16), "seq").astype(jnp.float32),
        lax.psum(shares[5].astype(jnp.bfloat16), "seq").astype(jnp.float32),
        lax.psum(shares[6].astype(jnp.bfloat16), "seq").astype(jnp.float32),
        lax.psum(shares[7].astype(jnp.bfloat16), "seq").astype(jnp.float32),
        lax.psum(shares[8].astype(jnp.bfloat16), "seq").astype(jnp.float32),
        lax.psum(shares[9].astype(jnp.bfloat16), "seq").astype(jnp.float32),
        lax.psum(shares[10].astype(jnp.bfloat16), "seq").astype(jnp.float32),
        lax.psum(shares[11].astype(jnp.bfloat16), "seq").astype(jnp.float32),
        lax.psum(shares[12].astype(jnp.bfloat16), "seq").astype(jnp.float32),
        lax.psum(shares[13].astype(jnp.bfloat16), "seq").astype(jnp.float32),
        lax.psum(shares[14].astype(jnp.bfloat16), "seq").astype(jnp.float32),
    )
    return (
        result.astype(jnp.bfloat16).reshape(shape_seq),
        grad_rows.reshape(shape_seq),
        summed_grads[0],
        summed_grads[1],
        summed_grads[2],
        summed_grads[3],
        summed_grads[4],
        summed_grads[5],
        summed_grads[6],
        summed_grads[7],
        summed_grads[8],
        summed_grads[9],
        summed_grads[10],
        summed_grads[11],
        summed_grads[12],
        summed_grads[13],
        summed_grads[14],
    )


def solution(mesh):
    return jax.shard_map(
        per_device,
        mesh=mesh,
        in_specs=(
            P("shard", "seq", None),
            P("shard"),
            P("shard", None),
            P("shard"),
            P("shard", None),
            P("shard", None),
            P("shard"),
            P("shard", None),
            P("shard"),
            P("shard"),
            P("shard"),
            P("shard", None),
            P("shard"),
            P("shard", None),
            P("shard"),
            P("shard"),
            P("shard"),
            P("shard", "seq", None),
        ),
        out_specs=(
            P("shard", "seq", None),
            P("shard", "seq", None),
            P("shard", None),
            P("shard"),
            P("shard", None),
            P("shard", None),
            P("shard"),
            P("shard", None),
            P("shard"),
            P("shard"),
            P("shard"),
            P("shard", None),
            P("shard"),
            P("shard", None),
            P("shard"),
            P("shard"),
            P("shard"),
        ),
        check_vma=False,
    )
```

profile of v0, /device:TPU:0, one launch (start us, length us, event | category | flops | bytes accessed | tf_op | source)
XLA Modules:
  0.0 1047.6 jit_solution(8084911402475072385)
XLA Ops:
  11.2 1.3 fusion.94
  19.8 39.2 %all-reduce.18 = (bf16[768]{0:T(1024)(128)(2,1)S(1)}, bf16[768]{0:T(1024)(128)(2,1)S(1)}, bf16[768]{0:T(1024)(128)(2,1)S(1)}, bf16[768]{0:T(1024)(128)(2,1)S(1)}...) all-reduce(bf16[768]{0:T(1024)(128)(2,1)S(1)} %dynamic-update-slice, ...), channel_id=1, replica_groups=mesh['shard'=8,'seq'=4] {'shard'}, use_global_device_ids=true, to_apply=%add.1 | all-reduce | flops 6144 | bytes 24576
  59.1 1.9 fusion.62
  61.0 1.1 copy.111
  62.1 3.5 all-to-all-start
  65.6 30.7 %all-gather.10.cloned.1.call-done = bf16[768,768]{1,0:T(8,128)(2,1)} async-done(((bf16[96,768]{1,0:T(8,128)(2,1)}), bf16[768,768]{1,0:T(8,128)(2,1)}) %all-gather.10.cloned.1.call-update) | async-done | bytes 1179664 | tf_op jit(solution)/shard_map/all_gather | solution.py:75
  96.3 1.7 fusion.63
  98.1 1.1 copy.114
  99.2 3.5 all-to-all-start.1
  102.6 35.7 %all-gather.12.cloned.1.call-done = bf16[768,768]{1,0:T(8,128)(2,1)} async-done(((bf16[96,768]{1,0:T(8,128)(2,1)}), bf16[768,768]{1,0:T(8,128)(2,1)}) %all-gather.12.cloned.1.call-update) | async-done | bytes 1179664 | tf_op jit(solution)/shard_map/all_gather | solution.py:77
  138.3 1.7 convolution_convert_fusion.1
  141.2 3.5 all-to-all-start.2
  145.7 6.3 all-to-all-done.2
  152.6 7.5 while.26
  161.2 3.5 all-to-all-start.3
  164.7 26.9 %all-gather = bf16[8,1,384]{2,1,0:T(2,128)(2,1)S(1)} all-gather(bf16[1,1,384]{2,1,0:T(2,128)(2,1)S(1)} %reshape.251), channel_id=1, replica_groups=mesh['shard'=8,'seq'=4] {'shard'}, dimensions={0}, use_global_device_ids=true | all-gather | bytes 6912 | tf_op jit(solution)/shard_map/all_gather | solution.py:85
  193.1 1.9 fusion.95
  195.3 65.1 %all-gather.16.cloned.1.call-done = bf16[768,3072]{1,0:T(8,128)(2,1)} async-done(((bf16[96,3072]{1,0:T(8,128)(2,1)}), bf16[768,3072]{1,0:T(8,128)(2,1)}) %all-gather.16.cloned.1.call-update) | async-done | bytes 4718608 | tf_op jit(solution)/shard_map/all_gather | solution.py:84
  260.4 11.7 %multiply_convert_fusion.1 = (bf16[256,3072]{1,0:T(8,128)(2,1)}, f32[256,3072]{1,0:T(8,128)}, f32[256,3072]{1,0:T(8,128)}) fusion(f32[3072]{0:T(1024)S(1)} %bitcast.275, bf16[768,3072]{1,0:T(8,128)(2,1)} %all-gather.16.cloned.1.call-done, f32[256,768]{1,0:T(8,128)S(1)} %get-tuple-element.290, f32[768]{0:T(1024)S(1)} %convert_element_type.217, ...), kind=kOutput, calls=%fused_computation.65 | convolution fusion | flops 1260847104 | bytes 13389824 | tf_op jit(solution)/shard_map/dot_general | solution.py:22
  272.1 68.0 %all-gather.18.cloned.1.call-done = bf16[3072,768]{1,0:T(8,128)(2,1)} async-done(((bf16[384,768]{1,0:T(8,128)(2,1)}), bf16[3072,768]{1,0:T(8,128)(2,1)}) %all-gather.18.cloned.1.call-update) | async-done | bytes 4718608 | tf_op jit(solution)/shard_map/all_gather | solution.py:86
  340.1 4.4 fusion.96
  345.3 1.1 fusion.92
  347.2 2.7 convert_reduce_fusion
  349.9 2.3 multiply_reduce_fusion.1
  352.2 1.1 fusion.91
  355.7 3.5 all-to-all-start.4
  359.2 1.9 fusion.75
  361.2 5.4 all-to-all-done.4
  367.9 14.8 %while.27 = (s32[]{:T(128)}, bf16[2,512,3,64]{1,3,2,0:T(8,128)(2,1)S(1)}, bf16[2,512,3,64]{1,3,2,0:T(8,128)(2,1)S(1)}, bf16[2,512,3,64]{1,3,2,0:T(8,128)(2,1)}, ...) while((s32[]{:T(128)}, ...), condition=%wide.region_14.15_spmd, body=%wide.region_12.14_spmd.sunk | while | flops 510884864 | bytes 28743872 | solution.py:200
  368.6 1.2 dynamic_slice.107
  376.0 1.2 dynamic_slice.107
  383.1 11.4 %all_to_all.120 = bf16[2,512,192]{2,0,1:T(2,128)(2,1)S(1)} all-to-all(bf16[2,512,192]{2,0,1:T(2,128)(2,1)S(1)} %copy.126), channel_id=1, replica_groups=mesh['shard'=8,'seq'=4] {'seq'}, dimensions={1} | all-to-all | bytes 786432 | tf_op jit(solution)/shard_map/all_to_all | solution.py:204
  397.5 2.0 copy.148
  399.6 1.3 copy.129
  400.9 11.2 %all_to_all.121 = bf16[2,512,192]{2,0,1:T(2,128)(2,1)S(1)} all-to-all(bf16[2,512,192]{2,0,1:T(2,128)(2,1)S(1)} %copy.129), channel_id=1, replica_groups=mesh['shard'=8,'seq'=4] {'seq'}, dimensions={1} | all-to-all | bytes 786432 | tf_op jit(solution)/shard_map/all_to_all | solution.py:205
  414.8 2.0 copy.150
  416.9 1.3 copy.132
  418.2 11.2 %all_to_all.122 = bf16[2,512,192]{2,0,1:T(2,128)(2,1)S(1)} all-to-all(bf16[2,512,192]{2,0,1:T(2,128)(2,1)S(1)} %copy.132), channel_id=1, replica_groups=mesh['shard'=8,'seq'=4] {'seq'}, dimensions={1} | all-to-all | bytes 786432 | tf_op jit(solution)/shard_map/all_to_all | solution.py:206
  432.4 2.0 copy.152
  434.4 1.3 copy-done.22
  435.7 6.4 fusion.88
  442.2 1.3 copy-done.15
  443.6 5.1 fusion.97
  451.2 35.3 %all-reduce.17 = (bf16[768]{0:T(1024)(128)(2,1)S(1)}, bf16[768]{0:T(1024)(128)(2,1)S(1)}, bf16[768]{0:T(1024)(128)(2,1)S(1)}, bf16[768]{0:T(1024)(128)(2,1)S(1)}...) all-reduce(f32[768]{0:T(1024)S(1)} %reduce_sum.190, ...), channel_id=3, replica_groups=mesh['shard'=8,'seq'=4] {'shard'}, use_global_device_ids=true, to_apply=%region_18.19.clone | all-reduce | flops 9216 | bytes 55296
  487.1 6.0 all-reduce.19
  497.8 1.6 convert_element_type.243
  499.5 4.9 reduce-scatter.19.cloned.1.call-done
  504.4 1.8 copy.149
  506.2 70.6 %reduce-scatter.21.cloned.1.call-done = f32[96,768]{1,0:T(8,128)} async-done(((f32[768,768]{1,0:T(8,128)}), f32[96,768]{1,0:T(8,128)}) %reduce-scatter.21.cloned.1.call-update) | async-done | bytes 294928
  576.8 1.8 copy.151
  578.5 70.5 %reduce-scatter.23.cloned.1.call-done = f32[96,768]{1,0:T(8,128)} async-done(((f32[768,768]{1,0:T(8,128)}), f32[96,768]{1,0:T(8,128)}) %reduce-scatter.23.cloned.1.call-update) | async-done | bytes 294928
  649.0 1.8 copy.153
  650.8 163.2 %reduce-scatter.15.cloned.1.call-done = f32[96,3072]{1,0:T(8,128)} async-done(((f32[768,3072]{1,0:T(8,128)}), f32[96,3072]{1,0:T(8,128)}) %reduce-scatter.15.cloned.1.call-update) | async-done | bytes 1179664 | tf_op jit(solution)/shard_map/reduce_scatter | solution.py:249
  814.0 2.2 convert_element_type.252
  816.1 162.6 %reduce-scatter.17.cloned.1.call-done = f32[384,768]{1,0:T(8,128)} async-done(((f32[3072,768]{1,0:T(8,128)}), f32[384,768]{1,0:T(8,128)}) %reduce-scatter.17.cloned.1.call-update) | async-done | bytes 1179664 | tf_op jit(solution)/shard_map/reduce_scatter | solution.py:251
  978.7 2.1 convert_element_type.257
  980.9 1.9 convolution_add_fusion.3
  983.4 1.4 convolution_add_fusion.1
  984.8 45.7 %all-reduce.23.cloned.1.call-done = (bf16[96,768]{0,1:T(8,128)(2,1)}, bf16[96,768]{0,1:T(8,128)(2,1)}, bf16[96,768]{0,1:T(8,128)(2,1)}, bf16[96,768]{1,0:T(8,128...) async-done(((bf16[96,768]{0,1:T(8,128)(2,1)}, bf16[96,768]{0,1:T(8,128)(2,1)}, bf16[96,768]{0,1:T(8,128)(2,1)}, bf16[96,768]{1,0:T(8,128)(2,1)}, ...) | async-done | bytes 1769488 | tf_op jit(solution)/shard_map/psum | solution.py:257
  1030.5 1.8 copy.137
  1032.3 1.8 copy.138
  1034.1 1.8 copy.139
  1035.9 1.6 convert_element_type.244
  1037.5 2.2 convert_element_type.253
  (251 shorter events, 58.1 us)
Async XLA Ops:
  7.2 89.1 %copy-start.1 = (bf16[2,128,768]{2,1,0:T(8,128)(2,1)S(1)}, bf16[2,128,768]{2,1,0:T(8,128)(2,1)}, u32[]{:S(2)}) copy-start(bf16[2,128,768]{2,1,0:T(8,128)(2,1)} %param.22) | copy-start | bytes 1179652
  7.2 51.9 %all-gather.8.cloned.1.call-start = ((), (), s32[]{:S(2)}) async-start(), calls=%async_computation.14 | async-start | bytes 1327104 | tf_op jit(solution)/shard_map/all_gather | solution.py:78
  7.9 88.4 %all-gather.10.cloned.1.call-start = ((), (), s32[]{:S(2)}) async-start(), calls=%async_computation.15 | async-start | bytes 1327104 | tf_op jit(solution)/shard_map/all_gather | solution.py:75
  8.7 129.7 %all-gather.12.cloned.1.call-start = ((), (), s32[]{:S(2)}) async-start(), calls=%async_computation.16 | async-start | bytes 1327104 | tf_op jit(solution)/shard_map/all_gather | solution.py:77
  9.4 183.7 %all-gather.14.cloned.1.call-start = ((), (), s32[]{:S(2)}) async-start(), calls=%async_computation.17 | async-start | bytes 1327104 | tf_op jit(solution)/shard_map/all_gather | solution.py:80
  10.0 250.4 %all-gather.16.cloned.1.call-start = ((), (), s32[]{:S(2)}) async-start(), calls=%async_computation.18 | async-start | bytes 5308416 | tf_op jit(solution)/shard_map/all_gather | solution.py:84
  10.6 329.6 %all-gather.18.cloned.1.call-start = ((), (), s32[]{:S(2)}) async-start(), calls=%async_computation.19 | async-start | bytes 5308416 | tf_op jit(solution)/shard_map/all_gather | solution.py:86
  62.1 37.1 %all-to-all-start = ((bf16[2,128,768]{1,0,2:T(2,128)(2,1)}), bf16[2,128,768]{1,0,2:T(2,128)(2,1)S(1)}, u32[]{:S(2)}, u32[]{:S(2)}) async-start(bf16[2,128,768]{1,0,2:T(2,128)(2,1)} %copy.111), calls=%async_computation | async-start | bytes 786432 | tf_op jit(solution)/shard_map/all_to_all | solution.py:120
  99.2 42.0 %all-to-all-start.1 = ((bf16[2,128,768]{1,0,2:T(2,128)(2,1)}), bf16[2,128,768]{1,0,2:T(2,128)(2,1)S(1)}, u32[]{:S(2)}, u32[]{:S(2)}) async-start(bf16[2,128,768]{1,0,2:T(2,128)(2,1)} %copy.114), calls=%async_computation.1 | async-start | bytes 786432 | tf_op jit(solution)/shard_map/all_to_all | solution.py:118
  141.2 10.8 %all-to-all-start.2 = ((bf16[2,128,768]{1,0,2:T(2,128)(2,1)}), bf16[2,128,768]{1,0,2:T(2,128)(2,1)S(1)}, u32[]{:S(2)}, u32[]{:S(2)}) async-start(bf16[2,128,768]{1,0,2:T(2,128)(2,1)} %copy.117), calls=%async_computation.2 | async-start | bytes 786432 | tf_op jit(solution)/shard_map/all_to_all | solution.py:119
  145.0 7.6 copy-start.37
  152.6 12.1 %copy-start.36 = (bf16[384]{0:T(512)(128)(2,1)S(1)}, bf16[384]{0:T(512)(128)(2,1)}, u32[]{:S(2)}) copy-start(bf16[384]{0:T(512)(128)(2,1)} %param.34) | copy-start | bytes 2308
  160.1 32.6 %copy-start.26 = (f32[2,3,512]{2,1,0:T(4,128)}, f32[2,3,512]{2,1,0:T(4,128)S(1)}, u32[]{:S(2)}) copy-start(f32[2,3,512]{2,1,0:T(4,128)S(1)} %get-tuple-element.438) | copy-start | bytes 36868
  161.2 30.5 %all-to-all-start.3 = ((bf16[2,512,192]{2,0,1:T(2,128)(2,1)}), bf16[2,512,192]{2,0,1:T(2,128)(2,1)S(1)}, u32[]{:S(2)}, u32[]{:S(2)}) async-start(bf16[2,512,192]{2,0,1:T(2,128)(2,1)} %copy.120), calls=%async_computation.3 | async-start | bytes 1048576 | tf_op jit(solution)/shard_map/all_to_all | solution.py:140
  195.0 157.2 %copy-start = (f32[256,768]{1,0:T(8,128)}, f32[256,768]{1,0:T(8,128)S(1)}, u32[]{:S(2)}) copy-start(f32[256,768]{1,0:T(8,128)S(1)} %get-tuple-element.290) | copy-start | bytes 2359300
  195.3 154.7 %copy-start.29 = (f32[256]{0:T(256)}, f32[256]{0:T(256)S(1)}, u32[]{:S(2)}) copy-start(f32[256]{0:T(256)S(1)} %fusion.86) | copy-start | bytes 3076
  340.1 7.0 slice-start.2
  340.1 4.7 copy-start.7
  340.1 7.0 slice-start.3
  340.1 7.0 copy-start.39
  344.6 2.6 copy-start.38
  346.4 3.5 slice-start
  347.1 2.8 copy-start.16
  347.2 2.8 slice-start.1
  349.9 2.3 copy-start.21
  352.2 1.9 copy-start.24
  353.3 0.7 copy-start.32
  355.7 10.8 %all-to-all-start.4 = ((bf16[2,128,768]{1,0,2:T(2,128)(2,1)}), bf16[2,128,768]{1,0,2:T(2,128)(2,1)S(1)}, u32[]{:S(2)}, u32[]{:S(2)}) async-start(bf16[2,128,768]{1,0,2:T(2,128)(2,1)} %copy.123), calls=%async_computation.4 | async-start | bytes 786432 | tf_op jit(solution)/shard_map/all_to_all | solution.py:169
  359.2 138.7 %reduce-scatter.13.cloned.1.call-start = ((), (), s32[]{:S(2)}) async-start(), calls=%async_computation.20 | async-start | bytes 2654208 | tf_op jit(solution)/shard_map/reduce_scatter | solution.py:245
  361.1 143.3 %reduce-scatter.19.cloned.1.call-start = ((), (), s32[]{:S(2)}) async-start(), calls=%async_computation.23 | async-start | bytes 2654208
  372.9 1.0 copy-start.19
  374.5 0.8 copy-start.20
  380.3 1.0 copy-start.19
  381.9 0.8 copy-start.20
  382.7 13.3 %copy-start.18 = (bf16[2,512,3,64]{1,3,2,0:T(8,128)(2,1)}, bf16[2,512,3,64]{1,3,2,0:T(8,128)(2,1)S(1)}, u32[]{:S(2)}) copy-start(bf16[2,512,3,64]{1,3,2,0:T(8,128)(2,1)S(1)} %get-tuple-element.112) | copy-start | bytes 1179652
  395.5 0.8 copy-start.9
  396.3 0.8 copy-start.13
  399.5 177.2 %reduce-scatter.21.cloned.1.call-start = ((), (), s32[]{:S(2)}) async-start(), calls=%async_computation.24 | async-start | bytes 2654208
  413.5 0.7 copy-start.3
  416.8 232.2 %reduce-scatter.23.cloned.1.call-start = ((), (), s32[]{:S(2)}) async-start(), calls=%async_computation.25 | async-start | bytes 2654208
  430.4 0.7 copy-start.11
  431.1 0.7 copy-start.5
  432.4 2.0 copy-start.30
  434.3 1.4 copy-start.22
  434.4 379.6 %reduce-scatter.15.cloned.1.call-start = ((), (), s32[]{:S(2)}) async-start(), calls=%async_computation.21 | async-start | bytes 10616832 | tf_op jit(solution)/shard_map/reduce_scatter | solution.py:249
  442.1 1.4 copy-start.15
  442.1 1.5 copy-start.17
  442.1 536.6 %reduce-scatter.17.cloned.1.call-start = ((), (), s32[]{:S(2)}) async-start(), calls=%async_computation.22 | async-start | bytes 10616832 | tf_op jit(solution)/shard_map/reduce_scatter | solution.py:251
  448.7 1.5 copy-start.8
  448.7 1.6 copy-start.10
  448.7 2.0 copy-start.12
  448.7 2.5 copy-start.27
  448.7 2.5 copy-start.28
  448.7 2.5 copy-start.31
  448.7 2.5 copy-start.34
  448.7 2.5 copy-start.35
  448.7 581.8 %all-reduce.23.cloned.1.call-start = ((), (), s32[]{:S(2)}) async-start(), calls=%async_computation.26 | async-start | bytes 3833856 | tf_op jit(solution)/shard_map/psum | solution.py:257
  506.2 474.7 %copy-start.14 = (bf16[2,128,4,192]{1,0,3,2:T(2,128)(2,1)S(1)}, bf16[2,128,4,192]{1,0,3,2:T(2,128)(2,1)}, u32[]{:S(2)}) copy-start(bf16[2,128,4,192]{1,0,3,2:T(2,128)(2,1)} %copy-done.13) | copy-start | bytes 1179652
  506.2 474.7 %copy-start.33 = (f32[256]{0:T(256)S(1)}, f32[256]{0:T(256)}, u32[]{:S(2)}) copy-start(f32[256]{0:T(256)} %copy-done.32) | copy-start | bytes 3076
  816.1 166.7 %copy-start.2 = (bf16[768,768]{1,0:T(8,128)(2,1)S(1)}, bf16[768,768]{1,0:T(8,128)(2,1)}, u32[]{:S(2)}) copy-start(bf16[768,768]{1,0:T(8,128)(2,1)} %all-gather.12.cloned.1.call-done) | copy-start | bytes 3538948
  816.1 166.7 %copy-start.4 = (bf16[2,128,4,192]{1,0,3,2:T(2,128)(2,1)S(1)}, bf16[2,128,4,192]{1,0,3,2:T(2,128)(2,1)}, u32[]{:S(2)}) copy-start(bf16[2,128,4,192]{1,0,3,2:T(2,128)(2,1)} %copy-done.3) | copy-start | bytes 1179652
  980.9 2.5 copy-start.6
  980.9 2.5 copy-start.23
  1030.5 9.2 copy-start.25
Sparse Core Ops, SparseCore 0:
  10.2 44.0 all-gather.7
  56.5 39.7 all-gather.9
  98.5 39.8 all-gather.11
  140.4 39.8 all-gather.13
  182.3 78.0 all-gather.15
  262.4 77.6 all-gather.17
  363.5 68.3 reduce-scatter.12
  435.4 68.9 reduce-scatter.18
  507.9 68.8 reduce-scatter.20
  580.1 68.8 reduce-scatter.22
  652.6 161.3 reduce-scatter.14
  817.4 161.2 reduce-scatter.16
  982.6 47.8 all-reduce.22
where the time goes:
time: 1060 us; the launch traced here: 1050 us
  waiting for transfers between devices  733 us (69%)
  blocking collectives  141 us (13%)
  matrix products  57.2 us (5%)
  local copies, waits for them, and re-layouts  55 us (5%)
  other arithmetic  26.5 us (2%)
  starting transfers between devices  17.8 us (2%)
  between operations  17.1 us (2%)
    reduce_scatter x1, waiting for transfers between devices, per_device(): lax.psum_scatter(local_grads[9], 'shard', scatter_dimension=0, tiled=True)  163 us
    reduce_scatter x1, waiting for transfers between devices, per_device(): lax.psum_scatter(local_grads[11], 'shard', scatter_dimension=0, tiled=True)  163 us
    unnamed x16, waiting for transfers between devices  150 us
    unnamed x2, blocking collectives  74.5 us
    all_gather x1, waiting for transfers between devices, per_device(): lax.all_gather(w_outer, 'shard', axis=0, tiled=True)  68 us
    all_gather x1, waiting for transfers between devices, per_device(): lax.all_gather(w_inner, 'shard', axis=0, tiled=True)  65.1 us
    psum x1, waiting for transfers between devices, per_device(): lax.psum(shares[0].astype(jnp.bfloat16), 'seq').astype(jnp.float32)  45.7 us
    all_gather x1, waiting for transfers between devices, per_device(): lax.all_gather(w_key, 'shard', axis=0, tiled=True)  35.7 us
  transfers between devices with their start and end apart: 18, of which 12 were waited for; matrix products, arithmetic and copies ran while one was open for 10% of the time, Pallas kernels for 0%

commit v1 on v0

--- a/solution.py
+++ b/solution.py
@@ -1,11 +1,16 @@
 from functools import partial
+from types import SimpleNamespace
 
 import jax
 import jax.numpy as jnp
 from jax import lax
+from jax.experimental import pallas as pl
+from jax.experimental.pallas import tpu as pltpu
 from jax.sharding import PartitionSpec as P
 
 HEAD_DIM = 64
+BF16, F32 = jnp.bfloat16, jnp.float32
+MESH = pl.DeviceIdType.MESH
 
 
 epsilon = 1e-12
@@ -38,6 +43,966 @@
     return jnp.sum(tensor.astype(jnp.float32), axis=0)
 
 
+def place():
+    shard, seq = lax.axis_index("shard"), lax.axis_index("seq")
+    return shard // 2, lax.rem(shard, 2), seq // 2, lax.rem(seq, 2)
+
+
+def device(z, x, y, core):
+    return (z * 2 + x, y * 2 + core)
+
+
+def send(src, dst, send_sem, recv_sem, where):
+    copy = pltpu.make_async_remote_copy(
+        src_ref=src,
+        dst_ref=dst,
+        send_sem=send_sem,
+        recv_sem=recv_sem,
+        device_id=where,
+        device_id_type=MESH,
+    )
+    copy.start()
+    return copy
+
+
+def await_bytes(ref, sem):
+    pltpu.make_async_copy(ref, ref, sem).wait()
+
+
+def greet(z, x, y, core):
+    barrier = pltpu.get_barrier_semaphore()
+    others = [device(lax.rem(z + j, 4), x, y, core) for j in (1, 2, 3)]
+    others += [device(z, 1 - x, y, core), device(z, x, 1 - y, core), device(z, x, y, 1 - core)]
+    for other in others:
+        pl.semaphore_signal(barrier, inc=1, device_id=other, device_id_type=MESH)
+    pl.semaphore_wait(barrier, len(others))
+
+
+def at(start, size):
+    return pl.ds(pl.multiple_of(start, size), size)
+
+
+ITEMS = [(0, 0), (1, 0), (2, 0), (3, 0)] + [(4, i) for i in range(4)] + [(5, i) for i in range(4)]
+SIXTH = 16
+LEAD = 2
+X_STEP = 2
+FORWARD_DELAY = (1, 2, 3)
+BACKWARD_DELAY = (0, 1, 2, 3, 4, 5)
+ROWS = 96
+
+
+def item_rows(ref, item, shard, start, size):
+    which, part = item
+    if which < 4:
+        return ref.at[at(shard * ROWS + start, size), :]
+    if which == 4:
+        return ref.at[at(shard * ROWS + start, size), pl.ds(part * 768, 768)]
+    return ref.at[at(shard * 4 * ROWS + part * ROWS + start, size), :]
+
+
+def column(start, width):
+    return pl.ds(pl.multiple_of(start, 128), width)
+
+
+def head_masks():
+    lane = lax.broadcasted_iota(jnp.int32, (1, 128), 1)
+    low = (lane < HEAD_DIM).astype(F32)
+    return (low.astype(BF16), (1.0 - low).astype(BF16))
+
+
+def vectors(r):
+    r.vec[...] = jnp.sum(r.small[...].astype(F32), axis=0)
+    for i in range(4):
+        r.b_inner[:, i * 768 : i * 768 + 768] = r.vec[5 + i : 6 + i, :]
+
+
+def project_one(r, name):
+    own = at(r.seq * 128, 128)
+    for slot in range(2):
+
+        @pl.loop(0, 3)
+        def _(c):
+            cols = column(c * 256, 256)
+            if name == "q":
+                r.q[slot, :, cols] = (product(r.x[slot, own, :], r.w_q[:, cols]) + r.vec[0:1, cols]).astype(BF16)
+            elif name == "k":
+                r.k[slot, :, cols] = product(r.x[slot], r.w_k[:, cols]).astype(BF16)
+            else:
+                r.v[slot, :, cols] = (product(r.x[slot], r.w_v[:, cols]) + r.vec[1:2, cols]).astype(BF16)
+
+
+def attend(r, slot, first, last):
+    masks = head_masks()
+    visible = lax.broadcasted_iota(jnp.int32, (512, 128), 0) < r.lengths[slot]
+
+    @pl.loop(first, last)
+    def _(p):
+        cols = column(p * 128, 128)
+        k, q, v = r.k[slot, :, cols], r.q[slot, :, cols], r.v[slot, :, cols]
+        context = None
+        for h in range(2):
+            scores = times_transposed(k, q * masks[h]) * (HEAD_DIM**-0.5)
+            logits = jnp.where(visible, scores, -1000000000.0)
+            shifted = jnp.exp(logits - jnp.max(logits, axis=0, keepdims=True))
+            probs = shifted * (1.0 / jnp.sum(shifted, axis=0, keepdims=True))
+            low = probs.astype(BF16)
+            r.p[slot, p * 2 + h] = low
+            part = row_contract(low, v * masks[h])
+            context = part if context is None else context + part
+        r.c[slot, :, cols] = context.astype(BF16)
+
+
+def norm_stats(rows):
+    average = jnp.mean(rows, axis=-1, keepdims=True)
+    centred = rows - average
+    variance = jnp.mean(centred * centred, axis=-1, keepdims=True)
+    scale = lax.rsqrt(variance + epsilon)
+    return centred * scale, scale
+
+
+def norm_back(grad, gain, unit, scale):
+    g = grad * gain
+    return scale * (
+        g - jnp.mean(g, axis=-1, keepdims=True) - unit * jnp.mean(g * unit, axis=-1, keepdims=True)
+    )
+
+
+def first_norm(r):
+    for slot in range(2):
+        rows = pl.ds(slot * 128, 128)
+        h1 = r.x[slot, at(r.seq * 128, 128), :].astype(F32) + product(r.c[slot], r.w_o[...]) + r.vec[2:3, :]
+        unit, scale = norm_stats(h1)
+        r.unit_one[rows, :] = unit
+        r.scale_one[rows, :] = jnp.broadcast_to(scale, (128, 128))
+        n1 = unit * r.vec[3:4, :] + r.vec[4:5, :]
+        r.n1[rows, :] = n1
+        r.n1b[rows, :] = n1.astype(BF16)
+
+
+def feed_in(r, i):
+    @pl.loop(0, 3)
+    def _(c):
+        cols = column(i * 768 + c * 256, 256)
+        u = product(r.n1b[...], r.w_inner[:, cols]) + r.b_inner[:, cols]
+        phi = 0.5 * (1.0 + lax.erf(u * 0.7071067811865476))
+        r.g[:, cols] = (u * phi).astype(BF16)
+        r.slope[:, cols] = (phi + u * (0.3989422804014327 * jnp.exp(-0.5 * u * u))).astype(BF16)
+
+
+def second_norm(r):
+    for slot in range(2):
+        rows = pl.ds(slot * 128, 128)
+        h2 = r.n1[rows, :] + product(r.g[rows, :], r.w_outer[...]) + r.vec[9:10, :]
+        unit, scale = norm_stats(h2)
+        r.result[slot] = (unit * r.vec[10:11, :] + r.vec[11:12, :]).astype(BF16)
+        grad = r.cot[slot].astype(F32)
+        back = norm_back(grad, r.vec[10:11, :], unit, scale)
+        low = back.astype(BF16)
+        r.dh2[rows, :] = back
+        r.df[rows, :] = low
+        tally(r, slot, 10, grad * unit)
+        tally(r, slot, 11, grad)
+        tally(r, slot, 9, low.astype(F32))
+
+
+def tally(r, slot, row, values):
+    total = jnp.sum(values, axis=0, keepdims=True)
+    r.sums[row : row + 1, :] = total if slot == 0 else r.sums[row : row + 1, :] + total
+
+
+KINDS = {
+    "place": ((16, 768), F32),
+    "small_own": ((16, 768), BF16),
+    "small": ((8, 16, 768), BF16),
+    "b_inner": ((1, 3072), F32),
+    "x": ((2, 512, 768), BF16),
+    "q": ((2, 128, 768), BF16),
+    "k": ((2, 512, 768), BF16),
+    "v": ((2, 512, 768), BF16),
+    "p": ((2, 12, 512, 128), BF16),
+    "c": ((2, 128, 768), BF16),
+    "unit_one": ((256, 768), F32),
+    "scale_one": ((256, 128), F32),
+    "n1": ((256, 768), F32),
+    "n1b": ((256, 768), BF16),
+    "g": ((256, 3072), BF16),
+    "slope": ((256, 3072), BF16),
+    "dh2": ((256, 768), F32),
+    "df": ((256, 768), BF16),
+    "da": ((2, 128, 768), BF16),
+    "dc": ((2, 128, 768), BF16),
+    "dq": ((2, 128, 768), BF16),
+    "dk": ((2, 512, 768), BF16),
+    "dv": ((2, 512, 768), BF16),
+    "dx_own": ((2, 128, 768), F32),
+    "dx_part": ((2, 512, 768), BF16),
+    "sums": ((16, 768), F32),
+    "ring": ((4, 768, 768), BF16),
+}
+
+
+def kinds(*names):
+    return {name: KINDS[name] for name in names}
+
+
+VECTOR_ROWS = (0, 1, 2, 3, 4, None, 9, 10, 11)
+HANDED = ("x", "q", "k", "v", "p", "c", "unit_one", "scale_one", "n1b", "g", "slope", "dh2", "df")
+
+FORWARD_WORK = kinds(
+    "place", "small_own", "small", "b_inner", "x", "q", "k", "v", "p", "c", "unit_one", "scale_one", "n1", "n1b", "g",
+    "slope", "dh2", "df",
+)
+
+def place_vectors(r, shard):
+    r.place[...] = jnp.zeros_like(r.place)
+    for row, ref in zip(VECTOR_ROWS, r.vectors):
+        if row is not None:
+            r.place[row : row + 1, 0:ROWS] = ref[...].astype(F32)
+    r.place[...] = pltpu.roll(r.place[...], shard * ROWS, 1)
+    r.place[pl.ds(5 + shard // 2, 1), column(lax.rem(shard, 2) * 384, 384)] = r.vectors[5][...].astype(F32)
+    r.small_own[...] = r.place[...].astype(BF16)
+
+
+def forward_kernel(*refs):
+    own = refs[0:6]
+    r = SimpleNamespace(vectors=refs[6:15])
+    x_own, r.cot, r.lengths = refs[15:18]
+    kept = refs[18:24]
+    r.result, r.sums, r.vec = refs[24:27]
+    handed = dict(zip(HANDED, refs[27:40]))
+    full = refs[40:46]
+    rest = list(refs[46:])
+    for name in FORWARD_WORK:
+        setattr(r, name, rest.pop(0))
+    r.w_q, r.w_k, r.w_v, r.w_o, r.w_inner, r.w_outer = full
+    small_own, small_full, x_full = r.small_own, r.small, r.x
+    send_sem, z_sem, x_sem, y_sem, c_sem, local_sem, extra_send, extra_recv, keep_sem = rest
+    z, x, y, core = place()
+    shard = z * 2 + x
+    seq = y * 2 + core
+    r.seq = seq
+    place_vectors(r, shard)
+    r.sums[...] = jnp.zeros_like(r.sums)
+    greet(z, x, y, core)
+    to_x = device(z, 1 - x, y, core)
+    to_y = device(z, x, 1 - y, core)
+    to_c = device(z, x, y, 1 - core)
+    offsets = (y * 64 + core * 16, 32 + core * 16)
+    far = (1 - y) * 64 + core * 16
+
+    def shard_at(back, side):
+        return lax.rem(z + 4 - back, 4) * 2 + side
+
+    def own_rows(item, off, size):
+        which, part = item
+        if which < 4:
+            return own[which].at[at(off, size), :]
+        if which == 4:
+            return own[which].at[at(off, size), pl.ds(part * 768, 768)]
+        return own[which].at[at(part * ROWS + off, size), :]
+
+    mine = x_full.at[:, at(seq * 128, 128), :]
+    x_local = pltpu.make_async_copy(x_own, mine, local_sem.at[6])
+    x_local.start()
+    s_local = pltpu.make_async_copy(small_own, small_full.at[shard], local_sem.at[7])
+    s_local.start()
+
+    def start(n):
+        item = ITEMS[n]
+        w = full[item[0]]
+        for piece, off in enumerate(offsets):
+            src = own_rows(item, off, SIXTH)
+            dst = item_rows(w, item, shard, off, SIXTH)
+            for j in (2, 1, 3):
+                send(src, dst, send_sem.at[n], z_sem.at[n, j - 1, piece], device(lax.rem(z + j, 4), x, y, core))
+            send(src, dst, send_sem.at[n], x_sem.at[n, 0, piece], to_x)
+
+    start(0)
+    send(x_own, mine, extra_send.at[0], extra_recv.at[0], to_y)
+    send(x_own, mine, extra_send.at[0], extra_recv.at[1], to_c)
+    for j in (1, 2, 3):
+        there = device(lax.rem(z + j, 4), x, y, core)
+        send(small_own, small_full.at[shard], extra_send.at[1], extra_recv.at[1 + j], there)
+    send(small_own, small_full.at[shard], extra_send.at[1], extra_recv.at[5], to_x)
+    for n in range(1, LEAD):
+        start(n)
+    locals_ = []
+    for w in range(6):
+        rows = own[w].shape[0]
+        copy = pltpu.make_async_copy(own[w], full[w].at[at(shard * rows, rows), :], local_sem.at[w])
+        copy.start()
+        locals_.append(copy)
+
+    def from_z(n):
+        item = ITEMS[n]
+        w = full[item[0]]
+        for j in (1, 2, 3):
+            for piece, off in enumerate(offsets):
+                got = item_rows(w, item, shard_at(j, x), off, SIXTH)
+                await_bytes(got, z_sem.at[n, j - 1, piece])
+                send(got, got, send_sem.at[n], x_sem.at[n, j, piece], to_x)
+                if piece == 0:
+                    send(got, got, send_sem.at[n], y_sem.at[n, j - 1], to_y)
+                send(got, got, send_sem.at[n], c_sem.at[n], to_c)
+
+    def from_x(n):
+        item = ITEMS[n]
+        w = full[item[0]]
+        for j in range(4):
+            for piece, off in enumerate(offsets):
+                got = item_rows(w, item, shard_at(j, 1 - x), off, SIXTH)
+                await_bytes(got, x_sem.at[n, j, piece])
+                if piece == 0:
+                    send(got, got, send_sem.at[n], y_sem.at[n, 3 + j], to_y)
+                send(got, got, send_sem.at[n], c_sem.at[n], to_c)
+
+    def from_y(n):
+        item = ITEMS[n]
+        w = full[item[0]]
+        for m in range(7):
+            owner = shard_at(m + 1, x) if m < 3 else shard_at(m - 3, 1 - x)
+            got = item_rows(w, item, owner, far, SIXTH)
+            await_bytes(got, y_sem.at[n, m])
+            send(got, got, send_sem.at[n], c_sem.at[n], to_c)
+
+    def from_c(n):
+        await_bytes(full[0].at[pl.ds(0, 7 * ROWS // 2), :], c_sem.at[n])
+
+    def small_relay():
+        for j in (1, 2, 3):
+            there = small_full.at[shard_at(j, x)]
+            await_bytes(there, extra_recv.at[1 + j])
+            send(there, there, extra_send.at[1], extra_recv.at[5 + j], to_x)
+
+    def x_relay():
+        theirs = x_full.at[:, at(((1 - y) * 2 + core) * 128, 128), :]
+        await_bytes(theirs, extra_recv.at[0])
+        send(theirs, theirs, extra_send.at[0], extra_recv.at[1], to_c)
+
+    keeps = []
+
+    def keep(src, dst):
+        copy = pltpu.make_async_copy(src, dst, keep_sem.at[len(keeps)])
+        copy.start()
+        keeps.append(copy)
+
+    def hand(*names):
+        for name in names:
+            keep(getattr(r, name), handed[name])
+
+    def arrive():
+        for j in range(4):
+            await_bytes(small_full.at[shard_at(j, 1 - x)], extra_recv.at[5 + j])
+        await_bytes(x_full.at[:, pl.ds(0, 256), :], extra_recv.at[1])
+        for copy in locals_:
+            copy.wait()
+        x_local.wait()
+        s_local.wait()
+        vectors(r)
+        hand("x")
+
+    def after(n):
+        if n == 0:
+            arrive()
+            project_one(r, "q")
+            hand("q")
+        elif n == 1:
+            project_one(r, "k")
+            hand("k")
+        elif n == 2:
+            project_one(r, "v")
+            hand("v")
+        if 2 <= n <= 5:
+            attend(r, (n - 2) // 2, (n % 2) * 3, (n % 2) * 3 + 3)
+        if n == 5:
+            hand("p", "c")
+            first_norm(r)
+            hand("unit_one", "scale_one", "n1b")
+            feed_in(r, 0)
+        if n == 6:
+            feed_in(r, 1)
+            feed_in(r, 2)
+        if n == 7:
+            feed_in(r, 3)
+            hand("g", "slope")
+        if n in (0, 1, 2, 3, 7, 11):
+            which = ITEMS[n][0]
+            keep(full[which], kept[which])
+
+    delay = FORWARD_DELAY
+    stages = ((0, from_z), (delay[0], from_x), (delay[1], from_y), (delay[2], from_c))
+    for step in range(len(ITEMS) + delay[2]):
+        if step + LEAD < len(ITEMS):
+            start(step + LEAD)
+        if step == 1:
+            small_relay()
+        if step == X_STEP:
+            x_relay()
+        for depth, stage in stages:
+            n = step - depth
+            if 0 <= n < len(ITEMS):
+                stage(n)
+        n = step - delay[2]
+        if 0 <= n < len(ITEMS):
+            after(n)
+
+    second_norm(r)
+    hand("dh2", "df")
+    await_bytes(x_full.at[:, pl.ds(0, 384), :], extra_send.at[0])
+    await_bytes(small_full.at[pl.ds(0, 7)], extra_send.at[1])
+    for n in range(len(ITEMS)):
+        await_bytes(full[0].at[pl.ds(0, 7 * ROWS), :], send_sem.at[n])
+    for copy in keeps:
+        copy.wait()
+
+
+def forward(weights, vectors_in, inputs, cotangent, lengths):
+    count = len(ITEMS)
+    wholes = [(8 * w.shape[0], w.shape[1]) for w in weights]
+    outs = [jax.ShapeDtypeStruct(shape, BF16) for shape in wholes]
+    outs += [
+        jax.ShapeDtypeStruct(cotangent.shape, BF16),
+        jax.ShapeDtypeStruct((16, 768), F32),
+        jax.ShapeDtypeStruct((16, 768), F32),
+    ]
+    outs += [jax.ShapeDtypeStruct(*FORWARD_WORK[name]) for name in HANDED]
+    vmem, anywhere = pl.BlockSpec(memory_space=pltpu.VMEM), pl.BlockSpec(memory_space=pl.ANY)
+    return pl.pallas_call(
+        forward_kernel,
+        out_shape=outs,
+        in_specs=[vmem] * 17 + [pl.BlockSpec(memory_space=pltpu.SMEM)],
+        out_specs=[anywhere] * 6 + [vmem] * 3 + [anywhere] * len(HANDED),
+        scratch_shapes=[pltpu.VMEM(shape, BF16) for shape in wholes]
+        + [pltpu.VMEM(*kind) for kind in FORWARD_WORK.values()]
+        + [
+            pltpu.SemaphoreType.DMA((count,)),
+            pltpu.SemaphoreType.DMA((count, 3, 2)),
+            pltpu.SemaphoreType.DMA((count, 4, 2)),
+            pltpu.SemaphoreType.DMA((count, 7)),
+            pltpu.SemaphoreType.DMA((count,)),
+            pltpu.SemaphoreType.DMA((8,)),
+            pltpu.SemaphoreType.DMA((2,)),
+            pltpu.SemaphoreType.DMA((9,)),
+            pltpu.SemaphoreType.DMA((6 + len(HANDED),)),
+        ],
+        compiler_params=pltpu.CompilerParams(
+            collective_id=0, has_side_effects=True, vmem_limit_bytes=60 * 2**20
+        ),
+        name="forward",
+    )(*weights, *vectors_in, inputs, cotangent, lengths)
+
+
+ORDER = (8, 9, 10, 11, 4, 5, 6, 7, 3, 0, 1, 2)
+RING = 4
+TAKE_ORDER = ("g", "df", "slope", "n1b", "dh2", "unit_one", "scale_one", "c", "k", "q", "v", "p", "x")
+GRAD_SHAPES = [(768, 768)] * 4 + [(768, 3072), (3072, 768)]
+
+BACKWARD_WORK = kinds(
+    "x", "q", "k", "v", "p", "c", "unit_one", "scale_one", "n1b", "g", "slope", "dh2", "df", "da", "dc", "dq", "dk", "dv",
+    "dx_own", "dx_part", "sums", "ring",
+)
+
+def ring_load(r, j):
+    if j < 4:
+        src = r.w_outer.at[pl.ds(j * 768, 768), :]
+    elif j < 8:
+        src = r.w_inner.at[:, pl.ds((j - 4) * 768, 768)]
+    else:
+        src = (r.w_o, r.w_q, r.w_k, r.w_v)[j - 8]
+    copy = pltpu.make_async_copy(src, r.ring.at[j % RING], r.ring_sem.at[j])
+    copy.start()
+    return copy
+
+
+def outer_grads(r):
+    @pl.loop(0, 12)
+    def _(c):
+        cols = column(c * 256, 256)
+        r.grads[5][at(c * 256, 256), :] = row_contract(r.g[:, cols], r.df[...]).astype(BF16)
+
+
+def inner_part(r, i, weight):
+    @pl.loop(0, 3)
+    def _(c):
+        cols = column(i * 768 + c * 256, 256)
+        low = (times_transposed(r.df[...], weight[at(c * 256, 256), :]) * r.slope[:, cols].astype(F32)).astype(BF16)
+        r.slope[:, cols] = low
+        r.sums[5 + i : 6 + i, column(c * 256, 256)] = jnp.sum(low.astype(F32), axis=0, keepdims=True)
+        r.grads[4][:, cols] = row_contract(r.n1b[...], low).astype(BF16)
+
+
+def normed_part(r, i, weight):
+    r.dh2[...] = r.dh2[...] + times_transposed(r.slope[:, i * 768 : i * 768 + 768], weight[...])
+
+
+def first_norm_back(r):
+    for slot in range(2):
+        rows = pl.ds(slot * 128, 128)
+        dn1 = r.dh2[rows, :]
+        unit = r.unit_one[rows, :]
+        back = norm_back(dn1, r.vec[3:4, :], unit, r.scale_one[rows, 0:1])
+        low = back.astype(BF16)
+        r.da[slot] = low
+        tally(r, slot, 3, dn1 * unit)
+        tally(r, slot, 4, dn1)
+        tally(r, slot, 2, low.astype(F32))
+        r.dx_own[slot] = back
+
+
+def output_back(r, weight):
+    for slot in range(2):
+        r.dc[slot] = times_transposed(r.da[slot], weight[...]).astype(BF16)
+
+
+def attend_back(r, slot, first, last):
+    masks = head_masks()
+    factor = HEAD_DIM**-0.5
+
+    @pl.loop(first, last)
+    def _(p):
+        cols = column(p * 128, 128)
+        k, q, v, dc = r.k[slot, :, cols], r.q[slot, :, cols], r.v[slot, :, cols], r.dc[slot, :, cols]
+        dq = dk = dv = None
+        for h in range(2):
+            low = r.p[slot, p * 2 + h]
+            probs = low.astype(F32)
+            dch = dc * masks[h]
+            dp = times_transposed(v, dch)
+            inner = jnp.sum(dp * probs, axis=0, keepdims=True)
+            ds = (probs * (dp - inner)).astype(BF16)
+            parts = (row_contract(ds, k * masks[h]), product(ds, q * masks[h]), product(low, dch))
+            dq, dk, dv = parts if dq is None else (dq + parts[0], dk + parts[1], dv + parts[2])
+        dq = (dq * factor).astype(BF16)
+        dv = dv.astype(BF16)
+        r.dq[slot, :, cols] = dq
+        r.dk[slot, :, cols] = (dk * factor).astype(BF16)
+        r.dv[slot, :, cols] = dv
+        dq_sum = jnp.sum(dq.astype(F32), axis=0, keepdims=True)
+        dv_sum = jnp.sum(dv.astype(F32), axis=0, keepdims=True)
+        if slot == 0:
+            r.sums[0:1, cols] = dq_sum
+            r.sums[1:2, cols] = dv_sum
+        else:
+            r.sums[0:1, cols] = r.sums[0:1, cols] + dq_sum
+            r.sums[1:2, cols] = r.sums[1:2, cols] + dv_sum
+
+
+def square_grad(r, which):
+    own = at(r.seq * 128, 128)
+
+    @pl.loop(0, 3)
+    def _(c):
+        cols = column(c * 256, 256)
+        value = None
+        for s in range(2):
+            left, right = (
+                (r.x[s, own, cols], r.dq[s]),
+                (r.x[s, :, cols], r.dk[s]),
+                (r.x[s, :, cols], r.dv[s]),
+                (r.c[s, :, cols], r.da[s]),
+            )[which]
+            piece = row_contract(left, right)
+            value = piece if value is None else value + piece
+        r.grads[which][at(c * 256, 256), :] = value.astype(BF16)
+
+
+def input_grads(r, w_q, w_k, w_v):
+    for slot in range(2):
+        r.dx_own[slot] = r.dx_own[slot] + times_transposed(r.dq[slot], w_q[...])
+
+        @pl.loop(0, 3)
+        def _(c):
+            rows = at(c * 256, 256)
+            r.dx_part[slot, :, column(c * 256, 256)] = (
+                times_transposed(r.dk[slot], w_k[rows, :]) + times_transposed(r.dv[slot], w_v[rows, :])
+            ).astype(BF16)
+
+
+def backward_kernel(*refs):
+    r = SimpleNamespace()
+    r.w_q, r.w_k, r.w_v, r.w_o, r.w_inner, r.w_outer = refs[0:6]
+    taken = dict(zip(HANDED, refs[6:19]))
+    r.vec, sums_in = refs[19:21]
+    out = refs[21:27]
+    small_out, dx_out = refs[27:29]
+    r.grads = refs[29:35]
+    rest = list(refs[35:])
+    for name in BACKWARD_WORK:
+        setattr(r, name, rest.pop(0))
+    (from_core, from_y, from_x, from_z, total, both, back_y, back_c) = rest[0:8]
+    (small_c, small_y, small_x, small_z, small_1, small_2, small_3, dx_c, dx_sum, dx_y) = rest[8:18]
+    send_sem, c_sem, y_sem, x_sem, z_sem, fy_sem, fc_sem, s_send, s_recv, d_send, d_recv = rest[18:29]
+    r.take_sem, r.ring_sem = rest[29:31]
+    f32 = F32
+    small = r.sums
+    z, x, y, core = place()
+    seq = y * 2 + core
+    r.seq = seq
+    takes = {}
+    for i, name in enumerate(TAKE_ORDER):
+        if name == "slope":
+            loads = [ring_load(r, j) for j in range(RING)]
+        takes[name] = pltpu.make_async_copy(taken[name], getattr(r, name), r.take_sem.at[i])
+        takes[name].start()
+    r.sums[...] = sums_in[...]
+    greet(z, x, y, core)
+    to_x = device(z, 1 - x, y, core)
+    to_y = device(z, x, 1 - y, core)
+    to_c = device(z, x, y, 1 - core)
+    mine = (y * 64 + core * 16, 32 + core * 16, (1 - y) * 64 + core * 16)
+    theirs = (y * 64 + (1 - core) * 16, 32 + (1 - core) * 16, (1 - y) * 64 + (1 - core) * 16)
+
+    def grad(n, start, shard):
+        item = ITEMS[ORDER[n]]
+        return item_rows(r.grads[item[0]], item, shard, start, SIXTH)
+
+    def to_partner(n):
+        for p in range(3):
+            for shard in range(8):
+                send(
+                    grad(n, theirs[p], shard),
+                    from_core.at[n, shard, pl.ds(p * 16, 16), :],
+                    send_sem.at[n],
+                    c_sem.at[n],
+                    to_c,
+                )
+
+    def stage_core(n):
+        await_bytes(from_core.at[n], c_sem.at[n])
+        for p in (2, 1):
+            for shard in range(8):
+                own = grad(n, mine[p], shard)
+                own[...] = (
+                    own[...].astype(f32) + from_core[n, shard, p * 16 : p * 16 + 16, :].astype(f32)
+                ).astype(BF16)
+                if p == 2:
+                    send(own, from_y.at[n, shard], send_sem.at[n], y_sem.at[n], to_y)
+
+    def stage_y(n):
+        await_bytes(from_y.at[n], y_sem.at[n])
+        for shard in range(8):
+            own = grad(n, mine[0], shard)
+            own[...] = (
+                own[...].astype(f32)
+                + from_core[n, shard, 0:16, :].astype(f32)
+                + from_y[n, shard].astype(f32)
+            ).astype(BF16)
+        for row in range(4):
+            for p in range(2):
+                send(
+                    grad(n, mine[p], row * 2 + 1 - x),
+                    from_x.at[n, row, pl.ds(p * 16, 16), :],
+                    send_sem.at[n],
+                    x_sem.at[n],
+                    to_x,
+                )
+
+    def stage_x(n):
+        await_bytes(from_x.at[n], x_sem.at[n])
+        for row in range(4):
+            for p in range(2):
+                own = grad(n, mine[p], row * 2 + x)
+                own[...] = (own[...].astype(f32) + from_x[n, row, p * 16 : p * 16 + 16, :].astype(f32)).astype(BF16)
+        for j in (2, 1, 3):
+            there = lax.rem(z + j, 4)
+            for p in range(2):
+                send(
+                    grad(n, mine[p], there * 2 + x),
+                    from_z.at[n, j - 1, pl.ds(p * 16, 16), :],
+                    send_sem.at[n],
+                    z_sem.at[n, j - 1],
+                    device(there, x, y, core),
+                )
+
+    def stage_z(n):
+        for j in range(3):
+            await_bytes(from_z.at[n, j], z_sem.at[n, j])
+        for p in range(2):
+            rows = pl.ds(p * 16, 16)
+            total[n, rows, :] = (
+                grad(n, mine[p], z * 2 + x)[...].astype(f32)
+                + from_z[n, 0, rows, :].astype(f32)
+                + from_z[n, 1, rows, :].astype(f32)
+                + from_z[n, 2, rows, :].astype(f32)
+            ).astype(BF16)
+        send(total.at[n], back_y.at[n], send_sem.at[n], fy_sem.at[n], to_y)
+        send(total.at[n, pl.ds(0, 16), :], back_c.at[n, pl.ds(0, 16), :], send_sem.at[n], fc_sem.at[n], to_c)
+
+    def put(n, start, value):
+        which, part = ITEMS[ORDER[n]]
+        rows = at(start + (part * ROWS if which == 5 else 0), SIXTH)
+        if which == 4:
+            out[which][rows, part * 768 : part * 768 + 768] = value
+        else:
+            out[which][rows, :] = value
+
+    def stage_back(n):
+        await_bytes(back_y.at[n], fy_sem.at[n])
+        both[n] = (total[n, 16:32, :].astype(f32) + back_y[n, 16:32, :].astype(f32)).astype(BF16)
+        send(both.at[n], back_c.at[n, pl.ds(16, 16), :], send_sem.at[n], fc_sem.at[n], to_c)
+        send(back_y.at[n, pl.ds(0, 16), :], back_c.at[n, pl.ds(32, 16), :], send_sem.at[n], fc_sem.at[n], to_c)
+        put(n, mine[0], total[n, 0:16, :])
+        put(n, mine[1], both[n])
+        put(n, mine[2], back_y[n, 0:16, :])
+
+    def stage_end(n):
+        await_bytes(back_c.at[n], fc_sem.at[n])
+        for p in range(3):
+            put(n, theirs[p], back_c[n, p * 16 : p * 16 + 16, :])
+
+    def dx_rows(who):
+        return r.dx_part.at[:, at(who * 128, 128), :]
+
+    def dx_0():
+        send(dx_rows((1 - y) * 2 + 1 - core), dx_c.at[1], d_send, d_recv.at[0], to_c)
+        send(dx_rows(y * 2 + 1 - core), dx_c.at[0], d_send, d_recv.at[0], to_c)
+
+    def dx_1():
+        await_bytes(dx_c, d_recv.at[0])
+        dx_sum[...] = (dx_rows((1 - y) * 2 + core)[...].astype(f32) + dx_c[1].astype(f32)).astype(BF16)
+        send(dx_sum, dx_y, d_send, d_recv.at[1], to_y)
+
+    def dx_end():
+        await_bytes(dx_y, d_recv.at[1])
+        dx_out[...] = (
+            r.dx_own[...] + dx_rows(seq)[...].astype(f32) + dx_c[0].astype(f32) + dx_y[...].astype(f32)
+        )
+
+    def small_0():
+        send(small, small_c, s_send.at[0], s_recv.at[0], to_c)
+
+    def small_1st():
+        await_bytes(small_c, s_recv.at[0])
+        small_1[...] = small[...] + small_c[...]
+        send(small_1, small_y, s_send.at[1], s_recv.at[1], to_y)
+
+    def small_2nd():
+        await_bytes(small_y, s_recv.at[1])
+        small_2[...] = small_1[...] + small_y[...]
+        send(small_2, small_x, s_send.at[2], s_recv.at[2], to_x)
+
+    def small_3rd():
+        await_bytes(small_x, s_recv.at[2])
+        small_3[...] = small_2[...] + small_x[...]
+        for j in (1, 2, 3):
+            send(small_3, small_z.at[z], s_send.at[3], s_recv.at[2 + j], device(lax.rem(z + j, 4), x, y, core))
+
+    def small_4th():
+        for j in (1, 2, 3):
+            await_bytes(small_z.at[lax.rem(z + 4 - j, 4)], s_recv.at[2 + j])
+        await_bytes(small_z.at[pl.ds(0, 3)], s_send.at[3])
+        small_z[z] = small_3[...]
+        small_out[...] = ((small_z[0] + small_z[1]) + small_z[2]) + small_z[3]
+
+    def block(j):
+        loads[j].wait()
+        return r.ring.at[j % RING]
+
+    def refill(j):
+        loads.append(ring_load(r, j))
+
+    def task(k):
+        if k == 0:
+            takes["g"].wait()
+            takes["df"].wait()
+            outer_grads(r)
+            for n in range(4):
+                to_partner(n)
+            takes["slope"].wait()
+            takes["n1b"].wait()
+        if k < 4:
+            inner_part(r, k, block(k))
+            refill(k + RING)
+            to_partner(4 + k)
+        if k == 4:
+            takes["dh2"].wait()
+            for i in range(4):
+                normed_part(r, i, block(4 + i))
+                refill(8 + i)
+            for name in ("unit_one", "scale_one", "c"):
+                takes[name].wait()
+            first_norm_back(r)
+            square_grad(r, 3)
+            to_partner(8)
+        if k == 5:
+            output_back(r, block(8))
+            for name in ("k", "q", "v", "p"):
+                takes[name].wait()
+        if 5 <= k <= 8:
+            attend_back(r, (k - 5) // 2, ((k - 5) % 2) * 3, ((k - 5) % 2) * 3 + 3)
+        if k == 9:
+            takes["x"].wait()
+            small_0()
+            for i in range(3):
+                square_grad(r, i)
+                to_partner(9 + i)
+        if k == 10:
+            input_grads(r, block(9), block(10), block(11))
+            dx_0()
+
+    extra = {10: small_1st, 11: small_2nd, 12: small_3rd, 14: small_4th}
+    count = len(ITEMS)
+    depths = BACKWARD_DELAY
+    stages = tuple(zip(depths, (stage_core, stage_y, stage_x, stage_z, stage_back, stage_end)))
+    for step in range(count + depths[-1]):
+        task(step)
+        for depth, stage in stages:
+            n = step - depth
+            if 0 <= n < count:
+                stage(n)
+        if step in extra:
+            extra[step]()
+        if step == 11:
+            dx_1()
+        if step == count + depths[-1] - 2:
+            dx_end()
+
+    for n in range(count):
+        await_bytes(from_core.at[n], send_sem.at[n])
+        await_bytes(from_y.at[n], send_sem.at[n])
+        await_bytes(from_x.at[n], send_sem.at[n])
+        await_bytes(from_z.at[n], send_sem.at[n])
+        await_bytes(back_y.at[n], send_sem.at[n])
+        await_bytes(back_c.at[n], send_sem.at[n])
+    for j in range(3):
+        await_bytes(small, s_send.at[j])
+    await_bytes(dx_c, d_send)
+    await_bytes(dx_sum, d_send)
+
+
+def backward(weights, handed, vec, sums, dx_like):
+    count = len(ITEMS)
+    outs = [jax.ShapeDtypeStruct((s[0] // 8, s[1]), BF16) for s in GRAD_SHAPES]
+    outs += [jax.ShapeDtypeStruct((16, 768), F32), jax.ShapeDtypeStruct(dx_like.shape, F32)]
+    vmem, anywhere = pl.BlockSpec(memory_space=pltpu.VMEM), pl.BlockSpec(memory_space=pl.ANY)
+    shape = (16, 768)
+    return pl.pallas_call(
+        backward_kernel,
+        out_shape=outs,
+        in_specs=[anywhere] * (6 + len(HANDED)) + [vmem] * 2,
+        out_specs=[vmem] * 8,
+        scratch_shapes=[pltpu.VMEM(s, BF16) for s in GRAD_SHAPES]
+        + [pltpu.VMEM(*kind) for kind in BACKWARD_WORK.values()]
+        + [
+            pltpu.VMEM((count, 8, 48, 768), BF16),
+            pltpu.VMEM((count, 8, 16, 768), BF16),
+            pltpu.VMEM((count, 4, 32, 768), BF16),
+            pltpu.VMEM((count, 3, 32, 768), BF16),
+            pltpu.VMEM((count, 32, 768), BF16),
+            pltpu.VMEM((count, 16, 768), BF16),
+            pltpu.VMEM((count, 32, 768), BF16),
+            pltpu.VMEM((count, 48, 768), BF16),
+        ]
+        + [pltpu.VMEM(shape, F32)] * 3
+        + [pltpu.VMEM((4,) + shape, F32)]
+        + [pltpu.VMEM(shape, F32)] * 3
+        + [
+            pltpu.VMEM((2,) + dx_like.shape, BF16),
+            pltpu.VMEM(dx_like.shape, BF16),
+            pltpu.VMEM(dx_like.shape, BF16),
+            pltpu.SemaphoreType.DMA((count,)),
+            pltpu.SemaphoreType.DMA((count,)),
+            pltpu.SemaphoreType.DMA((count,)),
+            pltpu.SemaphoreType.DMA((count,)),
+            pltpu.SemaphoreType.DMA((count, 3)),
+            pltpu.SemaphoreType.DMA((count,)),
+            pltpu.SemaphoreType.DMA((count,)),
+            pltpu.SemaphoreType.DMA((4,)),
+            pltpu.SemaphoreType.DMA((6,)),
+            pltpu.SemaphoreType.DMA,
+            pltpu.SemaphoreType.DMA((2,)),
+            pltpu.SemaphoreType.DMA((len(HANDED),)),
+            pltpu.SemaphoreType.DMA((12,)),
+        ],
+        compiler_params=pltpu.CompilerParams(
+            collective_id=1, has_side_effects=True, vmem_limit_bytes=67043328
+        ),
+        name="backward",
+    )(*weights, *handed, vec, sums)
+
+
+def finish_kernel(*refs):
+    shares, totals, dx, result = refs[0:6], refs[6], refs[7], refs[8]
+    outs = refs[9:15]
+    vectors_out = refs[15:24]
+    dx_out, result_out, turned = refs[24:27]
+    shard = lax.axis_index("shard")
+    for share, out in zip(shares, outs):
+        out[...] = share[...].astype(F32)
+    dx_out[...] = dx[...]
+    result_out[...] = result[...]
+    turned[...] = pltpu.roll(totals[...], lax.rem(8 - shard, 8) * ROWS, 1)
+    for row, out in zip(VECTOR_ROWS, vectors_out):
+        if row is not None:
+            out[...] = turned[row : row + 1, 0:ROWS]
+    vectors_out[5][...] = totals[pl.ds(5 + shard // 2, 1), column(lax.rem(shard, 2) * 384, 384)]
+
+
+def finish(shares, totals, dx, result):
+    outs = [jax.ShapeDtypeStruct(s.shape, F32) for s in shares]
+    outs += [jax.ShapeDtypeStruct((1, 384 if row is None else ROWS), F32) for row in VECTOR_ROWS]
+    outs += [jax.ShapeDtypeStruct(dx.shape, F32), jax.ShapeDtypeStruct(result.shape, BF16)]
+    vmem = pl.BlockSpec(memory_space=pltpu.VMEM)
+    return pl.pallas_call(
+        finish_kernel,
+        out_shape=outs,
+        in_specs=[vmem] * 9,
+        out_specs=[vmem] * len(outs),
+        scratch_shapes=[pltpu.VMEM((16, 768), F32)],
+        compiler_params=pltpu.CompilerParams(vmem_limit_bytes=32 * 2**20),
+        name="finish",
+    )(*shares, totals, dx, result)
+
+
+def per_device(
+    inputs,
+    lengths,
+    w_query,
+    b_query,
+    w_key,
+    w_value,
+    b_value,
+    w_output,
+    b_output,
+    gain_one,
+    shift_one,
+    w_inner,
+    b_inner,
+    w_outer,
+    b_outer,
+    gain_two,
+    shift_two,
+    cotangent,
+):
+    vectors_in = (b_query, b_value, b_output, gain_one, shift_one, b_inner, b_outer, gain_two, shift_two)
+    weights = (w_query, w_key, w_value, w_output, w_inner, w_outer)
+    first = forward(weights, [v.reshape(1, -1) for v in vectors_in], inputs, cotangent, lengths)
+    wholes, (result, sums, vec), handed = first[0:6], first[6:9], first[9:]
+    *shares, totals, dx = backward(wholes, handed, vec, sums, inputs)
+    done = finish(shares, totals, dx, result)
+    g_q, g_k, g_v, g_o, g_inner, g_outer = done[0:6]
+    g_bq, g_bv, g_bo, g_g1, g_s1, g_bi, g_bouter, g_g2, g_s2 = [v.reshape(-1) for v in done[6:15]]
+    return (
+        done[16],
+        done[15],
+        g_q,
+        g_bq,
+        g_k,
+        g_v,
+        g_bv,
+        g_o,
+        g_bo,
+        g_g1,
+        g_s1,
+        g_inner,
+        g_bi,
+        g_outer,
+        g_bouter,
+        g_g2,
+        g_s2,
+    )
+
+
 def head_logits(query_seq, key_seq, length, factor):
     scores = (
         jnp.einsum("qhd,khd->hqk", query_seq, key_seq, preferred_element_type=jnp.float32) * factor
@@ -46,7 +1011,7 @@
     return jnp.where(visible[None, None, :], scores, -1000000000.0)
 
 
-def per_device(
+def per_device_plain(
     inputs,
     lengths,
     w_query,
@@ -292,8 +1257,9 @@
 
 
 def solution(mesh):
+    tuned = (mesh.shape["shard"], mesh.shape["seq"]) == (8, 4)
     return jax.shard_map(
-        per_device,
+        per_device if tuned else per_device_plain,
         mesh=mesh,
         in_specs=(
             P("shard", "seq", None),

time: 1060 us -> 192 us (0.18); the launches traced: 1050 us -> 191 us
  waiting for transfers between devices: 733 us -> 0 us
  Pallas kernels: 0 us -> 180 us
  blocking collectives: 141 us -> 0 us
  matrix products: 57.2 us -> 0 us
  local copies, waits for them, and re-layouts: 55 us -> 9.93 us
  other arithmetic: 26.5 us -> 0.6 us
  starting transfers between devices: 17.8 us -> 0 us
  between operations: 17.1 us -> 0.69 us
    reduce_scatter x3 -> x0, waiting for transfers between devices: 326 us -> none  [the longest x1 163 us: per_device(): lax.psum_scatter(local_grads[9], 'shard', scatter_dimension=0, tiled=True)]
    all_gather x6 -> x0, waiting for transfers between devices: 200 us -> none  [the longest x1 68 us: per_device(): lax.all_gather(w_outer, 'shard', axis=0, tiled=True)]
    pallas_call x0 -> x3, Pallas kernels: none -> 180 us  [the longest x1 99.2 us: backward(): pl.pallas_call(backward_kernel, out_shape=outs, in_specs=[anywhere] * (6...]
    unnamed x16 -> x0, waiting for transfers between devices: 150 us -> none
    unnamed x2 -> x0, blocking collectives: 74.5 us -> none
    dot_general x32 -> x0, matrix products: 57.2 us -> none  [the longest x6 23.4 us: product(): return jnp.dot(operand, weight, preferred_element_type=jnp.float32)]
    psum x1 -> x0, waiting for transfers between devices: 45.7 us -> none  [per_device(): lax.psum(shares[0].astype(jnp.bfloat16), 'seq').astype(jnp.float32)]
    all_to_all x3 -> x0, blocking collectives: 33.8 us -> none  [the longest x1 11.4 us: per_device(): lax.all_to_all(head_gq.reshape(back_shape), 'seq', split_axis=1, concat_a...]
  transfers between devices with their start and end apart: 18 -> 0, of which waited for: 12 -> 0; matrix products, arithmetic and copies ran while one was open for 10% -> 0% of each run, Pallas kernels for 0% -> 0%
where the time goes in v1:
time: 192 us; the launch traced here: 191 us
  Pallas kernels  180 us (94%)
  local copies, waits for them, and re-layouts  9.93 us (5%)
    pallas_call x1, Pallas kernels, backward(): pl.pallas_call(backward_kernel, out_shape=outs, in_specs=[anywhere] * (6...  99.2 us
    pallas_call x1, Pallas kernels, forward(): pl.pallas_call(forward_kernel, out_shape=outs, in_specs=[vmem] * 17 + [pl...  78.6 us
    unnamed x18, local copies, waits for them, and re-layouts  8.68 us

profile of v1, /device:TPU:0, one launch (start us, length us, event | category | flops | bytes accessed | tf_op | source)
XLA Modules:
  0.0 191.2 jit_solution(12701649134361366001)
XLA Ops:
  0.7 1.2 reshape.93.refs_11_
  1.9 78.6 %forward.1 = (bf16[768,768]{1,0:T(8,128)(2,1)}, bf16[768,768]{1,0:T(8,128)(2,1)}, bf16[768,768]{1,0:T(8,128)(2,1)}, bf16[768,768]{1,0:T(8,128)(2,1)}, bf16[768,3...) custom-call(bf16[96,768]{1,0:T(8,128)(2,1)} %refs_0_.1, ...), custom_call_target="tpu_custom_call" | custom-call | tf_op jit(solution)/shard_map/forward/pallas_call | solution.py:470
  80.5 99.2 %backward.1 = (bf16[96,768]{1,0:T(8,128)(2,1)}, bf16[96,768]{1,0:T(8,128)(2,1)}, bf16[96,768]{1,0:T(8,128)(2,1)}, bf16[96,768]{1,0:T(8,128)(2,1)}, bf16[96,3072]...) custom-call(bf16[768,768]{1,0:T(8,128)(2,1)} %get-tuple-element.64.refs_0_, ...), custom_call_target="tpu_custom_call" | custom-call | tf_op jit(solution)/shard_map/backward/pallas_call | solution.py:879
  179.7 0.0 copy-start
  179.7 1.1 copy-done
  180.8 0.0 copy-start.1
  180.8 1.1 copy-done.1
  181.9 0.0 copy-start.2
  181.9 1.1 copy-done.2
  182.9 0.0 copy-start.3
  182.9 1.0 copy-done.3
  183.9 0.0 copy-start.4
  183.9 0.9 copy-done.4
  184.9 0.0 copy-start.5
  184.9 0.9 copy-done.5
  185.8 0.0 copy-start.6
  185.8 0.9 copy-done.6
  186.7 0.0 copy-start.7
  186.7 0.9 copy-done.7
  187.6 0.0 copy-start.8
  187.6 0.8 copy-done.8
  188.4 2.2 %finish.1 = (f32[96,768]{1,0:T(8,128)}, f32[96,768]{1,0:T(8,128)}, f32[96,768]{1,0:T(8,128)}, f32[96,768]{1,0:T(8,128)}, f32[96,3072]{1,0:T(8,128)}, /*index=5*/...) custom-call(bf16[96,768]{1,0:T(8,128)(2,1)S(1)} %copy-done.4, ...), custom_call_target="tpu_custom_call" | custom-call | tf_op jit(solution)/shard_map/finish/pallas_call | solution.py:946
  190.6 0.6 reduce
Async XLA Ops:
  179.7 1.1 copy-start
  180.8 1.1 copy-start.1
  181.9 1.1 copy-start.2
  182.9 1.0 copy-start.3
  183.9 0.9 copy-start.4
  184.9 0.9 copy-start.5
  185.8 0.9 copy-start.6
  186.7 0.9 copy-start.7
  187.6 0.8 copy-start.8

commit v2 on v1

--- a/solution.py
+++ b/solution.py
@@ -79,25 +79,23 @@
 
 
 def at(start, size):
-    return pl.ds(pl.multiple_of(start, size), size)
-
-
-ITEMS = [(0, 0), (1, 0), (2, 0), (3, 0)] + [(4, i) for i in range(4)] + [(5, i) for i in range(4)]
-SIXTH = 16
+    return pl.ds(pl.multiple_of(start, 16), size)
+
+
+ITEMS = [(w, 0, 768) for w in range(4)] + [(4, i * 768, 768) for i in range(4)] + [(5, i * 256, 256) for i in range(3)]
+ROWS = 96
+SHARD_ROWS = (96, 96, 96, 96, 96, 384)
+WIDTHS = (768, 768, 768, 768, 3072, 768)
 LEAD = 2
 X_STEP = 2
 FORWARD_DELAY = (1, 2, 3)
 BACKWARD_DELAY = (0, 1, 2, 3, 4, 5)
-ROWS = 96
-
-
-def item_rows(ref, item, shard, start, size):
-    which, part = item
-    if which < 4:
-        return ref.at[at(shard * ROWS + start, size), :]
-    if which == 4:
-        return ref.at[at(shard * ROWS + start, size), pl.ds(part * 768, 768)]
-    return ref.at[at(shard * 4 * ROWS + part * ROWS + start, size), :]
+THIRDS = (3,) * len(ITEMS)
+
+
+def half(item, core):
+    which, first, width = item
+    return pl.ds(pl.multiple_of(first + core * (width // 2), 128), width // 2)
 
 
 def column(start, width):
@@ -124,11 +122,11 @@
         def _(c):
             cols = column(c * 256, 256)
             if name == "q":
-                r.q[slot, :, cols] = (product(r.x[slot, own, :], r.w_q[:, cols]) + r.vec[0:1, cols]).astype(BF16)
+                r.q[slot, :, cols] = (product(r.x[slot, own, :], r.w_q[:, :, cols].reshape(768, 256)) + r.vec[0:1, cols]).astype(BF16)
             elif name == "k":
-                r.k[slot, :, cols] = product(r.x[slot], r.w_k[:, cols]).astype(BF16)
+                r.k[slot, :, cols] = product(r.x[slot], r.w_k[:, :, cols].reshape(768, 256)).astype(BF16)
             else:
-                r.v[slot, :, cols] = (product(r.x[slot], r.w_v[:, cols]) + r.vec[1:2, cols]).astype(BF16)
+                r.v[slot, :, cols] = (product(r.x[slot], r.w_v[:, :, cols].reshape(768, 256)) + r.vec[1:2, cols]).astype(BF16)
 
 
 def attend(r, slot, first, last):
@@ -170,7 +168,7 @@
 def first_norm(r):
     for slot in range(2):
         rows = pl.ds(slot * 128, 128)
-        h1 = r.x[slot, at(r.seq * 128, 128), :].astype(F32) + product(r.c[slot], r.w_o[...]) + r.vec[2:3, :]
+        h1 = r.x[slot, at(r.seq * 128, 128), :].astype(F32) + product(r.c[slot], r.w_o[...].reshape(768, 768)) + r.vec[2:3, :]
         unit, scale = norm_stats(h1)
         r.unit_one[rows, :] = unit
         r.scale_one[rows, :] = jnp.broadcast_to(scale, (128, 128))
@@ -183,17 +181,21 @@
     @pl.loop(0, 3)
     def _(c):
         cols = column(i * 768 + c * 256, 256)
-        u = product(r.n1b[...], r.w_inner[:, cols]) + r.b_inner[:, cols]
+        u = product(r.n1b[...], r.w_inner[:, :, cols].reshape(768, 256)) + r.b_inner[:, cols]
         phi = 0.5 * (1.0 + lax.erf(u * 0.7071067811865476))
         r.g[:, cols] = (u * phi).astype(BF16)
         r.slope[:, cols] = (phi + u * (0.3989422804014327 * jnp.exp(-0.5 * u * u))).astype(BF16)
 
 
+def feed_out(r, i):
+    cols = pl.ds(i * 256, 256)
+    r.dh2[:, cols] = r.n1[:, cols] + product(r.g[...], r.w_outer[:, :, cols].reshape(3072, 256)) + r.vec[9:10, cols]
+
+
 def second_norm(r):
     for slot in range(2):
         rows = pl.ds(slot * 128, 128)
-        h2 = r.n1[rows, :] + product(r.g[rows, :], r.w_outer[...]) + r.vec[9:10, :]
-        unit, scale = norm_stats(h2)
+        unit, scale = norm_stats(r.dh2[rows, :])
         r.result[slot] = (unit * r.vec[10:11, :] + r.vec[11:12, :]).astype(BF16)
         grad = r.cot[slot].astype(F32)
         back = norm_back(grad, r.vec[10:11, :], unit, scale)
@@ -276,7 +278,7 @@
         setattr(r, name, rest.pop(0))
     r.w_q, r.w_k, r.w_v, r.w_o, r.w_inner, r.w_outer = full
     small_own, small_full, x_full = r.small_own, r.small, r.x
-    send_sem, z_sem, x_sem, y_sem, c_sem, local_sem, extra_send, extra_recv, keep_sem = rest
+    send_sem, z_sem, x_sem, y_sem, c_sem, local_sem, own_sem, extra_send, extra_recv, keep_sem = rest
     z, x, y, core = place()
     shard = z * 2 + x
     seq = y * 2 + core
@@ -287,35 +289,37 @@
     to_x = device(z, 1 - x, y, core)
     to_y = device(z, x, 1 - y, core)
     to_c = device(z, x, y, 1 - core)
-    offsets = (y * 64 + core * 16, 32 + core * 16)
-    far = (1 - y) * 64 + core * 16
-
     def shard_at(back, side):
         return lax.rem(z + 4 - back, 4) * 2 + side
 
-    def own_rows(item, off, size):
-        which, part = item
-        if which < 4:
-            return own[which].at[at(off, size), :]
-        if which == 4:
-            return own[which].at[at(off, size), pl.ds(part * 768, 768)]
-        return own[which].at[at(part * ROWS + off, size), :]
+    def kept_rows(n):
+        rows = SHARD_ROWS[ITEMS[n][0]]
+        return rows, rows // 3
+
+    def block(n, owner, begin, size):
+        return full[ITEMS[n][0]].at[owner, at(begin, size), half(ITEMS[n], core)]
+
+    def carried(n, owner):
+        rows, third = kept_rows(n)
+        return block(n, owner, y * third, rows - third)
+
+    def for_y(n, owner):
+        rows, third = kept_rows(n)
+        return block(n, owner, y * (rows - third), third)
 
     mine = x_full.at[:, at(seq * 128, 128), :]
-    x_local = pltpu.make_async_copy(x_own, mine, local_sem.at[6])
+    x_local = pltpu.make_async_copy(x_own, mine, local_sem.at[0])
     x_local.start()
-    s_local = pltpu.make_async_copy(small_own, small_full.at[shard], local_sem.at[7])
+    s_local = pltpu.make_async_copy(small_own, small_full.at[shard], local_sem.at[1])
     s_local.start()
 
     def start(n):
-        item = ITEMS[n]
-        w = full[item[0]]
-        for piece, off in enumerate(offsets):
-            src = own_rows(item, off, SIXTH)
-            dst = item_rows(w, item, shard, off, SIXTH)
-            for j in (2, 1, 3):
-                send(src, dst, send_sem.at[n], z_sem.at[n, j - 1, piece], device(lax.rem(z + j, 4), x, y, core))
-            send(src, dst, send_sem.at[n], x_sem.at[n, 0, piece], to_x)
+        rows, third = kept_rows(n)
+        src = own[ITEMS[n][0]].at[at(y * third, rows - third), half(ITEMS[n], core)]
+        for j in (2, 1, 3):
+            there = device(lax.rem(z + j, 4), x, y, core)
+            send(src, carried(n, shard), send_sem.at[n], z_sem.at[n, j - 1], there)
+        send(src, carried(n, shard), send_sem.at[n], x_sem.at[n, 0], to_x)
 
     start(0)
     send(x_own, mine, extra_send.at[0], extra_recv.at[0], to_y)
@@ -327,46 +331,44 @@
     for n in range(1, LEAD):
         start(n)
     locals_ = []
-    for w in range(6):
-        rows = own[w].shape[0]
-        copy = pltpu.make_async_copy(own[w], full[w].at[at(shard * rows, rows), :], local_sem.at[w])
+    for n, item in enumerate(ITEMS):
+        rows = SHARD_ROWS[item[0]]
+        copy = pltpu.make_async_copy(own[item[0]].at[:, half(item, core)], block(n, shard, 0, rows), own_sem.at[n])
         copy.start()
         locals_.append(copy)
 
     def from_z(n):
-        item = ITEMS[n]
-        w = full[item[0]]
         for j in (1, 2, 3):
-            for piece, off in enumerate(offsets):
-                got = item_rows(w, item, shard_at(j, x), off, SIXTH)
-                await_bytes(got, z_sem.at[n, j - 1, piece])
-                send(got, got, send_sem.at[n], x_sem.at[n, j, piece], to_x)
-                if piece == 0:
-                    send(got, got, send_sem.at[n], y_sem.at[n, j - 1], to_y)
-                send(got, got, send_sem.at[n], c_sem.at[n], to_c)
+            owner = shard_at(j, x)
+            got = carried(n, owner)
+            await_bytes(got, z_sem.at[n, j - 1])
+            send(got, got, send_sem.at[n], x_sem.at[n, j], to_x)
+            send(for_y(n, owner), for_y(n, owner), send_sem.at[n], y_sem.at[n], to_y)
 
     def from_x(n):
-        item = ITEMS[n]
-        w = full[item[0]]
         for j in range(4):
-            for piece, off in enumerate(offsets):
-                got = item_rows(w, item, shard_at(j, 1 - x), off, SIXTH)
-                await_bytes(got, x_sem.at[n, j, piece])
-                if piece == 0:
-                    send(got, got, send_sem.at[n], y_sem.at[n, 3 + j], to_y)
-                send(got, got, send_sem.at[n], c_sem.at[n], to_c)
+            owner = shard_at(j, 1 - x)
+            await_bytes(carried(n, owner), x_sem.at[n, j])
+            send(for_y(n, owner), for_y(n, owner), send_sem.at[n], y_sem.at[n], to_y)
+
+    def some(n, owners, rows):
+        return full[ITEMS[n][0]].at[pl.ds(0, owners), pl.ds(0, rows), half(ITEMS[n], core)]
 
     def from_y(n):
-        item = ITEMS[n]
-        w = full[item[0]]
-        for m in range(7):
-            owner = shard_at(m + 1, x) if m < 3 else shard_at(m - 3, 1 - x)
-            got = item_rows(w, item, owner, far, SIXTH)
-            await_bytes(got, y_sem.at[n, m])
-            send(got, got, send_sem.at[n], c_sem.at[n], to_c)
+        rows, third = kept_rows(n)
+        await_bytes(some(n, 7, third), y_sem.at[n])
+        locals_[n].wait()
+        whole = some(n, 8, rows)
+        send(whole, whole, send_sem.at[n], c_sem.at[n], to_c)
 
     def from_c(n):
-        await_bytes(full[0].at[pl.ds(0, 7 * ROWS // 2), :], c_sem.at[n])
+        await_bytes(some(n, 8, SHARD_ROWS[ITEMS[n][0]]), c_sem.at[n])
+
+    def sent(n):
+        rows, third = kept_rows(n)
+        await_bytes(some(n, 7, rows - third), send_sem.at[n])
+        await_bytes(some(n, 7, third), send_sem.at[n])
+        await_bytes(some(n, 8, rows), send_sem.at[n])
 
     def small_relay():
         for j in (1, 2, 3):
@@ -394,8 +396,6 @@
         for j in range(4):
             await_bytes(small_full.at[shard_at(j, 1 - x)], extra_recv.at[5 + j])
         await_bytes(x_full.at[:, pl.ds(0, 256), :], extra_recv.at[1])
-        for copy in locals_:
-            copy.wait()
         x_local.wait()
         s_local.wait()
         vectors(r)
@@ -425,7 +425,9 @@
         if n == 7:
             feed_in(r, 3)
             hand("g", "slope")
-        if n in (0, 1, 2, 3, 7, 11):
+        if n >= 8:
+            feed_out(r, n - 8)
+        if n in (0, 1, 2, 3, 7, 10):
             which = ITEMS[n][0]
             keep(full[which], kept[which])
 
@@ -451,14 +453,14 @@
     await_bytes(x_full.at[:, pl.ds(0, 384), :], extra_send.at[0])
     await_bytes(small_full.at[pl.ds(0, 7)], extra_send.at[1])
     for n in range(len(ITEMS)):
-        await_bytes(full[0].at[pl.ds(0, 7 * ROWS), :], send_sem.at[n])
+        sent(n)
     for copy in keeps:
         copy.wait()
 
 
 def forward(weights, vectors_in, inputs, cotangent, lengths):
     count = len(ITEMS)
-    wholes = [(8 * w.shape[0], w.shape[1]) for w in weights]
+    wholes = [(8,) + w.shape for w in weights]
     outs = [jax.ShapeDtypeStruct(shape, BF16) for shape in wholes]
     outs += [
         jax.ShapeDtypeStruct(cotangent.shape, BF16),
@@ -476,11 +478,12 @@
         + [pltpu.VMEM(*kind) for kind in FORWARD_WORK.values()]
         + [
             pltpu.SemaphoreType.DMA((count,)),
-            pltpu.SemaphoreType.DMA((count, 3, 2)),
-            pltpu.SemaphoreType.DMA((count, 4, 2)),
-            pltpu.SemaphoreType.DMA((count, 7)),
+            pltpu.SemaphoreType.DMA((count, 3)),
+            pltpu.SemaphoreType.DMA((count, 4)),
             pltpu.SemaphoreType.DMA((count,)),
-            pltpu.SemaphoreType.DMA((8,)),
+            pltpu.SemaphoreType.DMA((count,)),
+            pltpu.SemaphoreType.DMA((2,)),
+            pltpu.SemaphoreType.DMA((count,)),
             pltpu.SemaphoreType.DMA((2,)),
             pltpu.SemaphoreType.DMA((9,)),
             pltpu.SemaphoreType.DMA((6 + len(HANDED),)),
@@ -492,10 +495,10 @@
     )(*weights, *vectors_in, inputs, cotangent, lengths)
 
 
-ORDER = (8, 9, 10, 11, 4, 5, 6, 7, 3, 0, 1, 2)
+ORDER = (8, 9, 10, 4, 5, 6, 7, 3, 0, 1, 2)
 RING = 4
 TAKE_ORDER = ("g", "df", "slope", "n1b", "dh2", "unit_one", "scale_one", "c", "k", "q", "v", "p", "x")
-GRAD_SHAPES = [(768, 768)] * 4 + [(768, 3072), (3072, 768)]
+GRAD_SHAPES = [(4, 2, rows, width) for rows, width in zip(SHARD_ROWS, WIDTHS)]
 
 BACKWARD_WORK = kinds(
     "x", "q", "k", "v", "p", "c", "unit_one", "scale_one", "n1b", "g", "slope", "dh2", "df", "da", "dc", "dq", "dk", "dv",
@@ -514,11 +517,11 @@
     return copy
 
 
-def outer_grads(r):
-    @pl.loop(0, 12)
-    def _(c):
-        cols = column(c * 256, 256)
-        r.grads[5][at(c * 256, 256), :] = row_contract(r.g[:, cols], r.df[...]).astype(BF16)
+def outer_grad(r, i):
+    cols = pl.ds(i * 256, 256)
+    for c in range(8):
+        left = r.g[:, c * 384 : c * 384 + 384]
+        r.grads[5][c // 2, c % 2, :, cols] = row_contract(left, r.df[:, cols]).astype(BF16)
 
 
 def inner_part(r, i, weight):
@@ -528,7 +531,7 @@
         low = (times_transposed(r.df[...], weight[at(c * 256, 256), :]) * r.slope[:, cols].astype(F32)).astype(BF16)
         r.slope[:, cols] = low
         r.sums[5 + i : 6 + i, column(c * 256, 256)] = jnp.sum(low.astype(F32), axis=0, keepdims=True)
-        r.grads[4][:, cols] = row_contract(r.n1b[...], low).astype(BF16)
+        r.grads[4][:, :, :, cols] = row_contract(r.n1b[...], low).astype(BF16).reshape(4, 2, ROWS, 256)
 
 
 def normed_part(r, i, weight):
@@ -590,9 +593,9 @@
 def square_grad(r, which):
     own = at(r.seq * 128, 128)
 
-    @pl.loop(0, 3)
+    @pl.loop(0, 2)
     def _(c):
-        cols = column(c * 256, 256)
+        cols = column(c * 384, 384)
         value = None
         for s in range(2):
             left, right = (
@@ -603,7 +606,7 @@
             )[which]
             piece = row_contract(left, right)
             value = piece if value is None else value + piece
-        r.grads[which][at(c * 256, 256), :] = value.astype(BF16)
+        r.grads[which][pl.ds(c * 2, 2)] = value.astype(BF16).reshape(2, 2, ROWS, 768)
 
 
 def input_grads(r, w_q, w_k, w_v):
@@ -629,10 +632,12 @@
     rest = list(refs[35:])
     for name in BACKWARD_WORK:
         setattr(r, name, rest.pop(0))
-    (from_core, from_y, from_x, from_z, total, both, back_y, back_c) = rest[0:8]
-    (small_c, small_y, small_x, small_z, small_1, small_2, small_3, dx_c, dx_sum, dx_y) = rest[8:18]
-    send_sem, c_sem, y_sem, x_sem, z_sem, fy_sem, fc_sem, s_send, s_recv, d_send, d_recv = rest[18:29]
-    r.take_sem, r.ring_sem = rest[29:31]
+    count = len(ITEMS)
+    from_core, from_y, from_x, from_z, total, back_y = [rest[i * count : i * count + count] for i in range(6)]
+    rest = rest[6 * count :]
+    (small_c, small_y, small_x, small_z, small_1, small_2, small_3, dx_c, dx_sum, dx_y) = rest[0:10]
+    send_sem, c_sem, y_sem, x_sem, z_sem, fy_sem, fc_sem, s_send, s_recv, d_send, d_recv = rest[10:21]
+    r.take_sem, r.ring_sem = rest[21:23]
     f32 = F32
     small = r.sums
     z, x, y, core = place()
@@ -649,106 +654,88 @@
     to_x = device(z, 1 - x, y, core)
     to_y = device(z, x, 1 - y, core)
     to_c = device(z, x, y, 1 - core)
-    mine = (y * 64 + core * 16, 32 + core * 16, (1 - y) * 64 + core * 16)
-    theirs = (y * 64 + (1 - core) * 16, 32 + (1 - core) * 16, (1 - y) * 64 + (1 - core) * 16)
-
-    def grad(n, start, shard):
+
+    def parts(n):
+        rows = SHARD_ROWS[ITEMS[ORDER[n]][0]]
+        return rows, rows // THIRDS[n]
+
+    def grad(n, side=core):
         item = ITEMS[ORDER[n]]
-        return item_rows(r.grads[item[0]], item, shard, start, SIXTH)
+        return r.grads[item[0]].at[:, :, :, half(item, side)]
 
     def to_partner(n):
-        for p in range(3):
-            for shard in range(8):
-                send(
-                    grad(n, theirs[p], shard),
-                    from_core.at[n, shard, pl.ds(p * 16, 16), :],
-                    send_sem.at[n],
-                    c_sem.at[n],
-                    to_c,
-                )
+        send(grad(n, 1 - core), from_core[n], send_sem.at[n], c_sem.at[n], to_c)
+
+    def add(ref, *others):
+        value = ref[...].astype(f32)
+        for other in others:
+            value = value + other[...].astype(f32)
+        ref[...] = value.astype(BF16)
 
     def stage_core(n):
-        await_bytes(from_core.at[n], c_sem.at[n])
-        for p in (2, 1):
-            for shard in range(8):
-                own = grad(n, mine[p], shard)
-                own[...] = (
-                    own[...].astype(f32) + from_core[n, shard, p * 16 : p * 16 + 16, :].astype(f32)
-                ).astype(BF16)
-                if p == 2:
-                    send(own, from_y.at[n, shard], send_sem.at[n], y_sem.at[n], to_y)
+        rows, part = parts(n)
+        await_bytes(from_core[n], c_sem.at[n])
+        far = at((1 - y) * (rows - part), part)
+        add(grad(n).at[:, :, far, :], from_core[n].at[:, :, far, :])
+        send(grad(n).at[:, :, far, :], from_y[n], send_sem.at[n], y_sem.at[n], to_y)
+        middle = pl.ds(part, rows - 2 * part)
+        add(grad(n).at[:, :, middle, :], from_core[n].at[:, :, middle, :])
 
     def stage_y(n):
-        await_bytes(from_y.at[n], y_sem.at[n])
-        for shard in range(8):
-            own = grad(n, mine[0], shard)
-            own[...] = (
-                own[...].astype(f32)
-                + from_core[n, shard, 0:16, :].astype(f32)
-                + from_y[n, shard].astype(f32)
-            ).astype(BF16)
-        for row in range(4):
-            for p in range(2):
-                send(
-                    grad(n, mine[p], row * 2 + 1 - x),
-                    from_x.at[n, row, pl.ds(p * 16, 16), :],
-                    send_sem.at[n],
-                    x_sem.at[n],
-                    to_x,
-                )
+        rows, part = parts(n)
+        await_bytes(from_y[n], y_sem.at[n])
+        near = at(y * (rows - part), part)
+        add(grad(n).at[:, :, near, :], from_core[n].at[:, :, near, :], from_y[n])
+        carried = at(y * part, rows - part)
+        send(grad(n).at[:, 1 - x, carried, :], from_x[n], send_sem.at[n], x_sem.at[n], to_x)
 
     def stage_x(n):
-        await_bytes(from_x.at[n], x_sem.at[n])
-        for row in range(4):
-            for p in range(2):
-                own = grad(n, mine[p], row * 2 + x)
-                own[...] = (own[...].astype(f32) + from_x[n, row, p * 16 : p * 16 + 16, :].astype(f32)).astype(BF16)
+        rows, part = parts(n)
+        await_bytes(from_x[n], x_sem.at[n])
+        carried = at(y * part, rows - part)
+        add(grad(n).at[:, x, carried, :], from_x[n])
         for j in (2, 1, 3):
             there = lax.rem(z + j, 4)
-            for p in range(2):
-                send(
-                    grad(n, mine[p], there * 2 + x),
-                    from_z.at[n, j - 1, pl.ds(p * 16, 16), :],
-                    send_sem.at[n],
-                    z_sem.at[n, j - 1],
-                    device(there, x, y, core),
-                )
+            send(
+                grad(n).at[there, x, carried, :],
+                from_z[n].at[j - 1],
+                send_sem.at[n],
+                z_sem.at[n, j - 1],
+                device(there, x, y, core),
+            )
 
     def stage_z(n):
+        rows, part = parts(n)
         for j in range(3):
-            await_bytes(from_z.at[n, j], z_sem.at[n, j])
-        for p in range(2):
-            rows = pl.ds(p * 16, 16)
-            total[n, rows, :] = (
-                grad(n, mine[p], z * 2 + x)[...].astype(f32)
-                + from_z[n, 0, rows, :].astype(f32)
-                + from_z[n, 1, rows, :].astype(f32)
-                + from_z[n, 2, rows, :].astype(f32)
-            ).astype(BF16)
-        send(total.at[n], back_y.at[n], send_sem.at[n], fy_sem.at[n], to_y)
-        send(total.at[n, pl.ds(0, 16), :], back_c.at[n, pl.ds(0, 16), :], send_sem.at[n], fc_sem.at[n], to_c)
-
-    def put(n, start, value):
-        which, part = ITEMS[ORDER[n]]
-        rows = at(start + (part * ROWS if which == 5 else 0), SIXTH)
-        if which == 4:
-            out[which][rows, part * 768 : part * 768 + 768] = value
-        else:
-            out[which][rows, :] = value
+            await_bytes(from_z[n].at[j], z_sem.at[n, j])
+        value = grad(n).at[z, x, at(y * part, rows - part), :][...].astype(f32)
+        for j in range(3):
+            value = value + from_z[n][j].astype(f32)
+        total[n][...] = value.astype(BF16)
+        send(total[n], back_y[n], send_sem.at[n], fy_sem.at[n], to_y)
+
+    def shares(n):
+        item = ITEMS[ORDER[n]]
+        return out[item[0]].at[:, half(item, core)]
 
     def stage_back(n):
-        await_bytes(back_y.at[n], fy_sem.at[n])
-        both[n] = (total[n, 16:32, :].astype(f32) + back_y[n, 16:32, :].astype(f32)).astype(BF16)
-        send(both.at[n], back_c.at[n, pl.ds(16, 16), :], send_sem.at[n], fc_sem.at[n], to_c)
-        send(back_y.at[n, pl.ds(0, 16), :], back_c.at[n, pl.ds(32, 16), :], send_sem.at[n], fc_sem.at[n], to_c)
-        put(n, mine[0], total[n, 0:16, :])
-        put(n, mine[1], both[n])
-        put(n, mine[2], back_y[n, 0:16, :])
+        rows, part = parts(n)
+        await_bytes(back_y[n], fy_sem.at[n])
+        middle = rows - 2 * part
+        place_ = shares(n)
+        place_[at(y * (rows - part), part), :] = total[n][at(y * middle, part), :]
+        place_[at((1 - y) * (rows - part), part), :] = back_y[n][at((1 - y) * middle, part), :]
+        place_[pl.ds(part, middle), :] = (
+            total[n][at((1 - y) * part, middle), :].astype(f32) + back_y[n][at(y * part, middle), :].astype(f32)
+        ).astype(BF16)
+        send(place_, place_, send_sem.at[n], fc_sem.at[n], to_c)
 
     def stage_end(n):
-        await_bytes(back_c.at[n], fc_sem.at[n])
-        for p in range(3):
-            put(n, theirs[p], back_c[n, p * 16 : p * 16 + 16, :])
+        await_bytes(shares(n), fc_sem.at[n])
+
+    def sent(n):
+        for ref in (from_core[n], from_y[n], from_x[n], from_z[n], total[n], shares(n)):
+            await_bytes(ref, send_sem.at[n])
 
     def dx_rows(who):
         return r.dx_part.at[:, at(who * 128, 128), :]
@@ -805,15 +792,18 @@
         if k == 0:
             takes["g"].wait()
             takes["df"].wait()
-            outer_grads(r)
-            for n in range(4):
-                to_partner(n)
+            for i in range(2):
+                outer_grad(r, i)
+                to_partner(i)
+        if k == 1:
+            outer_grad(r, 2)
+            to_partner(2)
             takes["slope"].wait()
             takes["n1b"].wait()
-        if k < 4:
-            inner_part(r, k, block(k))
-            refill(k + RING)
-            to_partner(4 + k)
+        for i in ((), (0,), (1,), (2, 3))[k] if k < 4 else ():
+            inner_part(r, i, block(i))
+            refill(i + RING)
+            to_partner(3 + i)
         if k == 4:
             takes["dh2"].wait()
             for i in range(4):
@@ -823,25 +813,24 @@
                 takes[name].wait()
             first_norm_back(r)
             square_grad(r, 3)
-            to_partner(8)
+            to_partner(7)
         if k == 5:
             output_back(r, block(8))
             for name in ("k", "q", "v", "p"):
                 takes[name].wait()
-        if 5 <= k <= 8:
-            attend_back(r, (k - 5) // 2, ((k - 5) % 2) * 3, ((k - 5) % 2) * 3 + 3)
-        if k == 9:
+        for i in {5: (0,), 6: (1,), 7: (2, 3)}.get(k, ()):
+            attend_back(r, i // 2, (i % 2) * 3, (i % 2) * 3 + 3)
+        if k == 8:
             takes["x"].wait()
             small_0()
             for i in range(3):
                 square_grad(r, i)
-                to_partner(9 + i)
-        if k == 10:
+                to_partner(8 + i)
+        if k == 9:
             input_grads(r, block(9), block(10), block(11))
             dx_0()
 
-    extra = {10: small_1st, 11: small_2nd, 12: small_3rd, 14: small_4th}
-    count = len(ITEMS)
+    extra = {9: small_1st, 10: small_2nd, 11: small_3rd, 13: small_4th}
     depths = BACKWARD_DELAY
     stages = tuple(zip(depths, (stage_core, stage_y, stage_x, stage_z, stage_back, stage_end)))
     for step in range(count + depths[-1]):
@@ -852,27 +841,35 @@
                 stage(n)
         if step in extra:
             extra[step]()
-        if step == 11:
+        if step == 10:
             dx_1()
         if step == count + depths[-1] - 2:
             dx_end()
 
     for n in range(count):
-        await_bytes(from_core.at[n], send_sem.at[n])
-        await_bytes(from_y.at[n], send_sem.at[n])
-        await_bytes(from_x.at[n], send_sem.at[n])
-        await_bytes(from_z.at[n], send_sem.at[n])
-        await_bytes(back_y.at[n], send_sem.at[n])
-        await_bytes(back_c.at[n], send_sem.at[n])
+        sent(n)
     for j in range(3):
         await_bytes(small, s_send.at[j])
     await_bytes(dx_c, d_send)
     await_bytes(dx_sum, d_send)
 
 
+def reduce_shapes():
+    stages = [[] for _ in range(6)]
+    for n, number in enumerate(ORDER):
+        which, _, width = ITEMS[number]
+        rows = SHARD_ROWS[which]
+        part, width = rows // THIRDS[n], width // 2
+        left = rows - part
+        shapes = ((4, 2, rows, width), (4, 2, part, width), (4, left, width), (3, left, width), (left, width), (left, width))
+        for stage, shape in zip(stages, shapes):
+            stage.append(shape)
+    return stages
+
+
 def backward(weights, handed, vec, sums, dx_like):
     count = len(ITEMS)
-    outs = [jax.ShapeDtypeStruct((s[0] // 8, s[1]), BF16) for s in GRAD_SHAPES]
+    outs = [jax.ShapeDtypeStruct(s[2:], BF16) for s in GRAD_SHAPES]
     outs += [jax.ShapeDtypeStruct((16, 768), F32), jax.ShapeDtypeStruct(dx_like.shape, F32)]
     vmem, anywhere = pl.BlockSpec(memory_space=pltpu.VMEM), pl.BlockSpec(memory_space=pl.ANY)
     shape = (16, 768)
@@ -883,16 +880,7 @@
         out_specs=[vmem] * 8,
         scratch_shapes=[pltpu.VMEM(s, BF16) for s in GRAD_SHAPES]
         + [pltpu.VMEM(*kind) for kind in BACKWARD_WORK.values()]
-        + [
-            pltpu.VMEM((count, 8, 48, 768), BF16),
-            pltpu.VMEM((count, 8, 16, 768), BF16),
-            pltpu.VMEM((count, 4, 32, 768), BF16),
-            pltpu.VMEM((count, 3, 32, 768), BF16),
-            pltpu.VMEM((count, 32, 768), BF16),
-            pltpu.VMEM((count, 16, 768), BF16),
-            pltpu.VMEM((count, 32, 768), BF16),
-            pltpu.VMEM((count, 48, 768), BF16),
-        ]
+        + [pltpu.VMEM(shape_, BF16) for stage in reduce_shapes() for shape_ in stage]
         + [pltpu.VMEM(shape, F32)] * 3
         + [pltpu.VMEM((4,) + shape, F32)]
         + [pltpu.VMEM(shape, F32)] * 3
@@ -949,7 +937,7 @@
         in_specs=[vmem] * 9,
         out_specs=[vmem] * len(outs),
         scratch_shapes=[pltpu.VMEM((16, 768), F32)],
-        compiler_params=pltpu.CompilerParams(vmem_limit_bytes=32 * 2**20),
+        compiler_params=pltpu.CompilerParams(vmem_limit_bytes=67043328),
         name="finish",
     )(*shares, totals, dx, result)
 
@@ -977,7 +965,8 @@
     vectors_in = (b_query, b_value, b_output, gain_one, shift_one, b_inner, b_outer, gain_two, shift_two)
     weights = (w_query, w_key, w_value, w_output, w_inner, w_outer)
     first = forward(weights, [v.reshape(1, -1) for v in vectors_in], inputs, cotangent, lengths)
-    wholes, (result, sums, vec), handed = first[0:6], first[6:9], first[9:]
+    wholes = [w.reshape(-1, w.shape[2]) for w in first[0:6]]
+    (result, sums, vec), handed = first[6:9], first[9:]
     *shares, totals, dx = backward(wholes, handed, vec, sums, inputs)
     done = finish(shares, totals, dx, result)
     g_q, g_k, g_v, g_o, g_inner, g_outer = done[0:6]

time: 192 us -> 177 us (0.922)
  local copies, waits for them, and re-layouts: 9.93 us -> 1.24 us
  Pallas kernels: 180 us -> 174 us
    unnamed x18 -> x0, local copies, waits for them, and re-layouts: 8.68 us -> none
    pallas_call x1, Pallas kernels: 99.2 us -> 91.6 us  [backward(): pl.pallas_call(backward_kernel, out_shape=outs, in_specs=[anywhere] * (6...]
where the time goes in v2:
time: 177 us
  Pallas kernels  174 us (98%)
    pallas_call x1, Pallas kernels, backward(): pl.pallas_call(backward_kernel, out_shape=outs, in_specs=[anywhere] * (6...  91.6 us
    pallas_call x1, Pallas kernels, forward(): pl.pallas_call(forward_kernel, out_shape=outs, in_specs=[vmem] * 17 + [pl...  77.9 us
    pallas_call x1, Pallas kernels, finish(): pl.pallas_call(finish_kernel, out_shape=outs, in_specs=[vmem] * 9, out_sp...  4.11 us

profile of v2, /device:TPU:0, one launch (start us, length us, event | category | flops | bytes accessed | tf_op | source)
XLA Modules:
  0.0 176.8 jit_solution(9049747167417430078)
XLA Ops:
  0.7 1.2 reshape.111.refs_11_
  1.9 77.9 %forward.1 = (bf16[8,96,768]{2,1,0:T(8,128)(2,1)}, bf16[8,96,768]{2,1,0:T(8,128)(2,1)}, bf16[8,96,768]{2,1,0:T(8,128)(2,1)}, bf16[8,96,768]{2,1,0:T(8,128)(2,1)}...) custom-call(bf16[96,768]{1,0:T(8,128)(2,1)} %refs_0_.1, ...), custom_call_target="tpu_custom_call" | custom-call | tf_op jit(solution)/shard_map/forward/pallas_call | solution.py:472
  79.8 91.6 %backward.1 = (bf16[96,768]{1,0:T(8,128)(2,1)}, bf16[96,768]{1,0:T(8,128)(2,1)}, bf16[96,768]{1,0:T(8,128)(2,1)}, bf16[96,768]{1,0:T(8,128)(2,1)}, bf16[96,3072]...) custom-call(bf16[768,768]{1,0:T(8,128)(2,1)} %bitcast.24, ...), custom_call_target="tpu_custom_call" | custom-call | tf_op jit(solution)/shard_map/backward/pallas_call | solution.py:876
  171.4 4.1 %finish.1 = (f32[96,768]{1,0:T(8,128)}, f32[96,768]{1,0:T(8,128)}, f32[96,768]{1,0:T(8,128)}, f32[96,768]{1,0:T(8,128)}, f32[96,3072]{1,0:T(8,128)}, /*index=5*/...) custom-call(bf16[96,768]{1,0:T(8,128)(2,1)} %get-tuple-element.85.re, ...), custom_call_target="tpu_custom_call" | custom-call | tf_op jit(solution)/shard_map/finish/pallas_call | solution.py:934
  175.5 1.3 reduce

commit v3 on v2

--- a/solution.py
+++ b/solution.py
@@ -69,6 +69,10 @@
     pltpu.make_async_copy(ref, ref, sem).wait()
 
 
+def along_z(z):
+    return (z + 1 - 2 * lax.rem(z, 2), lax.rem(z + 2, 4), 3 - z)
+
+
 def greet(z, x, y, core):
     barrier = pltpu.get_barrier_semaphore()
     others = [device(lax.rem(z + j, 4), x, y, core) for j in (1, 2, 3)]
@@ -88,8 +92,8 @@
 WIDTHS = (768, 768, 768, 768, 3072, 768)
 LEAD = 2
 X_STEP = 2
-FORWARD_DELAY = (1, 2, 3)
-BACKWARD_DELAY = (0, 1, 2, 3, 4, 5)
+FORWARD_DELAY = (1, 2, 4, 5)
+BACKWARD_DELAY = (0, 1, 2, 4, 5, 6)
 THIRDS = (3,) * len(ITEMS)
 
 
@@ -261,7 +265,7 @@
         if row is not None:
             r.place[row : row + 1, 0:ROWS] = ref[...].astype(F32)
     r.place[...] = pltpu.roll(r.place[...], shard * ROWS, 1)
-    r.place[pl.ds(5 + shard // 2, 1), column(lax.rem(shard, 2) * 384, 384)] = r.vectors[5][...].astype(F32)
+    r.place[pl.ds(5 + shard // 2, 1), column(lax.rem(shard, 2) * 384, 384)] = r.vectors[5][...].astype(F32).reshape(1, 384)
     r.small_own[...] = r.place[...].astype(BF16)
 
 
@@ -289,6 +293,8 @@
     to_x = device(z, 1 - x, y, core)
     to_y = device(z, x, 1 - y, core)
     to_c = device(z, x, y, 1 - core)
+    others = along_z(z)
+
     def shard_at(back, side):
         return lax.rem(z + 4 - back, 4) * 2 + side
 
@@ -316,9 +322,8 @@
     def start(n):
         rows, third = kept_rows(n)
         src = own[ITEMS[n][0]].at[at(y * third, rows - third), half(ITEMS[n], core)]
-        for j in (2, 1, 3):
-            there = device(lax.rem(z + j, 4), x, y, core)
-            send(src, carried(n, shard), send_sem.at[n], z_sem.at[n, j - 1], there)
+        for m in (1, 0):
+            send(src, carried(n, shard), send_sem.at[n], z_sem.at[n, m], device(others[m], x, y, core))
         send(src, carried(n, shard), send_sem.at[n], x_sem.at[n, 0], to_x)
 
     start(0)
@@ -337,17 +342,25 @@
         copy.start()
         locals_.append(copy)
 
+    def pass_on(n, m):
+        owner = others[m] * 2 + x
+        got = carried(n, owner)
+        await_bytes(got, z_sem.at[n, m])
+        if m == 1:
+            send(got, got, send_sem.at[n], z_sem.at[n, 2], device(others[0], x, y, core))
+        send(got, got, send_sem.at[n], x_sem.at[n, 1 + m], to_x)
+        send(for_y(n, owner), for_y(n, owner), send_sem.at[n], y_sem.at[n], to_y)
+
     def from_z(n):
-        for j in (1, 2, 3):
-            owner = shard_at(j, x)
-            got = carried(n, owner)
-            await_bytes(got, z_sem.at[n, j - 1])
-            send(got, got, send_sem.at[n], x_sem.at[n, j], to_x)
-            send(for_y(n, owner), for_y(n, owner), send_sem.at[n], y_sem.at[n], to_y)
+        pass_on(n, 0)
+        pass_on(n, 1)
+
+    def from_far_z(n):
+        pass_on(n, 2)
 
     def from_x(n):
         for j in range(4):
-            owner = shard_at(j, 1 - x)
+            owner = (z if j == 0 else others[j - 1]) * 2 + 1 - x
             await_bytes(carried(n, owner), x_sem.at[n, j])
             send(for_y(n, owner), for_y(n, owner), send_sem.at[n], y_sem.at[n], to_y)
 
@@ -432,8 +445,8 @@
             keep(full[which], kept[which])
 
     delay = FORWARD_DELAY
-    stages = ((0, from_z), (delay[0], from_x), (delay[1], from_y), (delay[2], from_c))
-    for step in range(len(ITEMS) + delay[2]):
+    stages = ((0, from_z),) + tuple(zip(delay, (from_far_z, from_x, from_y, from_c)))
+    for step in range(len(ITEMS) + delay[-1]):
         if step + LEAD < len(ITEMS):
             start(step + LEAD)
         if step == 1:
@@ -444,7 +457,7 @@
             n = step - depth
             if 0 <= n < len(ITEMS):
                 stage(n)
-        n = step - delay[2]
+        n = step - delay[-1]
         if 0 <= n < len(ITEMS):
             after(n)
 
@@ -923,12 +936,12 @@
     for row, out in zip(VECTOR_ROWS, vectors_out):
         if row is not None:
             out[...] = turned[row : row + 1, 0:ROWS]
-    vectors_out[5][...] = totals[pl.ds(5 + shard // 2, 1), column(lax.rem(shard, 2) * 384, 384)]
+    vectors_out[5][...] = totals[pl.ds(5 + shard // 2, 1), column(lax.rem(shard, 2) * 384, 384)].reshape(384)
 
 
 def finish(shares, totals, dx, result):
     outs = [jax.ShapeDtypeStruct(s.shape, F32) for s in shares]
-    outs += [jax.ShapeDtypeStruct((1, 384 if row is None else ROWS), F32) for row in VECTOR_ROWS]
+    outs += [jax.ShapeDtypeStruct((384,) if row is None else (1, ROWS), F32) for row in VECTOR_ROWS]
     outs += [jax.ShapeDtypeStruct(dx.shape, F32), jax.ShapeDtypeStruct(result.shape, BF16)]
     vmem = pl.BlockSpec(memory_space=pltpu.VMEM)
     return pl.pallas_call(
@@ -964,7 +977,7 @@
 ):
     vectors_in = (b_query, b_value, b_output, gain_one, shift_one, b_inner, b_outer, gain_two, shift_two)
     weights = (w_query, w_key, w_value, w_output, w_inner, w_outer)
-    first = forward(weights, [v.reshape(1, -1) for v in vectors_in], inputs, cotangent, lengths)
+    first = forward(weights, [v if v is b_inner else v.reshape(1, -1) for v in vectors_in], inputs, cotangent, lengths)
     wholes = [w.reshape(-1, w.shape[2]) for w in first[0:6]]
     (result, sums, vec), handed = first[6:9], first[9:]
     *shares, totals, dx = backward(wholes, handed, vec, sums, inputs)

time: 177 us -> 171 us (0.966)
  Pallas kernels: 174 us -> 170 us
    pallas_call x1, Pallas kernels: 77.9 us -> 75.5 us  [forward(): pl.pallas_call(forward_kernel, out_shape=outs, in_specs=[vmem] * 17 + [pl...]
where the time goes in v3:
time: 171 us; the launch traced here: 170 us
  Pallas kernels  170 us (99%)
    pallas_call x1, Pallas kernels, backward(): pl.pallas_call(backward_kernel, out_shape=outs, in_specs=[anywhere] * (6...  90.1 us
    pallas_call x1, Pallas kernels, forward(): pl.pallas_call(forward_kernel, out_shape=outs, in_specs=[vmem] * 17 + [pl...  75.5 us
    pallas_call x1, Pallas kernels, finish(): pl.pallas_call(finish_kernel, out_shape=outs, in_specs=[vmem] * 9, out_sp...  4.11 us

profile of v3, /device:TPU:0, one launch (start us, length us, event | category | flops | bytes accessed | tf_op | source)
XLA Modules:
  0.0 170.4 jit_solution(2110683912475208692)
XLA Ops:
  0.7 75.5 %forward.1 = (bf16[8,96,768]{2,1,0:T(8,128)(2,1)}, bf16[8,96,768]{2,1,0:T(8,128)(2,1)}, bf16[8,96,768]{2,1,0:T(8,128)(2,1)}, bf16[8,96,768]{2,1,0:T(8,128)(2,1)}...) custom-call(bf16[96,768]{1,0:T(8,128)(2,1)} %refs_0_.1, ...), custom_call_target="tpu_custom_call" | custom-call | tf_op jit(solution)/shard_map/forward/pallas_call | solution.py:485
  76.2 90.1 %backward.1 = (bf16[96,768]{1,0:T(8,128)(2,1)}, bf16[96,768]{1,0:T(8,128)(2,1)}, bf16[96,768]{1,0:T(8,128)(2,1)}, bf16[96,768]{1,0:T(8,128)(2,1)}, bf16[96,3072]...) custom-call(bf16[768,768]{1,0:T(8,128)(2,1)} %bitcast.24, ...), custom_call_target="tpu_custom_call" | custom-call | tf_op jit(solution)/shard_map/backward/pallas_call | solution.py:889
  166.2 4.1 %finish.1 = (f32[96,768]{1,0:T(8,128)}, f32[96,768]{1,0:T(8,128)}, f32[96,768]{1,0:T(8,128)}, f32[96,768]{1,0:T(8,128)}, f32[96,3072]{1,0:T(8,128)}, /*index=5*/...) custom-call(bf16[96,768]{1,0:T(8,128)(2,1)} %get-tuple-element.85.re, ...), custom_call_target="tpu_custom_call" | custom-call | tf_op jit(solution)/shard_map/finish/pallas_call | solution.py:947

commit v4 on v3

--- a/solution.py
+++ b/solution.py
@@ -92,8 +92,8 @@
 WIDTHS = (768, 768, 768, 768, 3072, 768)
 LEAD = 2
 X_STEP = 2
-FORWARD_DELAY = (1, 2, 4, 5)
-BACKWARD_DELAY = (0, 1, 2, 4, 5, 6)
+FORWARD_DELAY = (1, 3, 5, 6)
+BACKWARD_DELAY = (0, 2, 3, 5, 8, 9)
 THIRDS = (3,) * len(ITEMS)
 
 

time: 171 us -> 165 us (0.965)
  Pallas kernels: 170 us -> 164 us
    pallas_call x1, Pallas kernels: 90.1 us -> 85.6 us  [backward(): pl.pallas_call(backward_kernel, out_shape=outs, in_specs=[anywhere] * (6...]
where the time goes in v4:
time: 165 us
  Pallas kernels  164 us (99%)
    pallas_call x1, Pallas kernels, backward(): pl.pallas_call(backward_kernel, out_shape=outs, in_specs=[anywhere] * (6...  85.6 us
    pallas_call x1, Pallas kernels, forward(): pl.pallas_call(forward_kernel, out_shape=outs, in_specs=[vmem] * 17 + [pl...  74.7 us
    pallas_call x1, Pallas kernels, finish(): pl.pallas_call(finish_kernel, out_shape=outs, in_specs=[vmem] * 9, out_sp...  4.11 us

profile of v4, /device:TPU:0, one launch (start us, length us, event | category | flops | bytes accessed | tf_op | source)
XLA Modules:
  0.0 165.2 jit_solution(5496638076140113451)
XLA Ops:
  0.7 74.7 %forward.1 = (bf16[8,96,768]{2,1,0:T(8,128)(2,1)}, bf16[8,96,768]{2,1,0:T(8,128)(2,1)}, bf16[8,96,768]{2,1,0:T(8,128)(2,1)}, bf16[8,96,768]{2,1,0:T(8,128)(2,1)}...) custom-call(bf16[96,768]{1,0:T(8,128)(2,1)} %refs_0_.1, ...), custom_call_target="tpu_custom_call" | custom-call | tf_op jit(solution)/shard_map/forward/pallas_call | solution.py:485
  75.4 85.6 %backward.1 = (bf16[96,768]{1,0:T(8,128)(2,1)}, bf16[96,768]{1,0:T(8,128)(2,1)}, bf16[96,768]{1,0:T(8,128)(2,1)}, bf16[96,768]{1,0:T(8,128)(2,1)}, bf16[96,3072]...) custom-call(bf16[768,768]{1,0:T(8,128)(2,1)} %bitcast.24, ...), custom_call_target="tpu_custom_call" | custom-call | tf_op jit(solution)/shard_map/backward/pallas_call | solution.py:889
  161.0 4.1 %finish.1 = (f32[96,768]{1,0:T(8,128)}, f32[96,768]{1,0:T(8,128)}, f32[96,768]{1,0:T(8,128)}, f32[96,768]{1,0:T(8,128)}, f32[96,3072]{1,0:T(8,128)}, /*index=5*/...) custom-call(bf16[96,768]{1,0:T(8,128)(2,1)} %get-tuple-element.85.re, ...), custom_call_target="tpu_custom_call" | custom-call | tf_op jit(solution)/shard_map/finish/pallas_call | solution.py:947
